TPU v7x, 128 devices: a whole 4x4x4 slice. The times are simulated.
128 devices in a mesh: tm: 32 (over z, y, core), space: 4 (over x).
Axes of the slice: x: 4, y: 4, z: 4, core: 2. Of those that a mesh axis runs over, the one named last changes fastest.
Arguments:
- frames_in: bfloat16 [32, 256, 128, 128], P('tm', None, 'space'), may hold values from -6 to 6
- conv_weight: bfloat16 [3, 3, 256, 256], replicated, may hold values from -0.125 to 0.125
- out_weight: bfloat16 [256, 256], replicated, may hold values from -0.375 to 0.375
- skip_gain: float32 [256], replicated, may hold values from -4 to 4
- decays: float32 [32, 256], P('tm'), may hold values from 0.25 to 1, as said below
Outputs:
- frames_out: bfloat16 [32, 256, 128, 128], P('tm', None, 'space')
Inputs may be any that keep to these rules, and one draw needn't show every extreme that they name: `decays`: every entry lies strictly below 1.
All inputs are finite; a program needn't handle non-finite values.
Results may differ from a plain program's by a relative error of at most 0.0041.
Values may be sent and summed in bfloat16 or wider, within the bound.
A program may use at most 320 MiB of HBM per device.

v0:
```python
import jax
import jax.numpy as jnp
from jax import lax
from jax.sharding import PartitionSpec as P


def with_halo(block, sides, width):
    for axis, dim in sides:
        count = lax.axis_size(axis)
        forward = [(i, i + 1) for i in range(count - 1)]
        backward = [(target, source) for source, target in forward]
        low = lax.ppermute(
            lax.slice_in_dim(block, block.shape[dim] - width, None, axis=dim), axis, forward
        )
        high = lax.ppermute(lax.slice_in_dim(block, 0, width, axis=dim), axis, backward)
        block = jnp.concatenate([low, block, high], axis=dim)
    return block


def entering(array, axis, combine, identity):
    length, here = (lax.axis_size(axis), lax.axis_index(axis))
    everything = jax.tree.map(lambda part: lax.all_gather(part, axis), array)
    start = jax.tree.map(
        lambda part, zero: jnp.broadcast_to(jnp.asarray(zero, part.dtype), part.shape),
        array,
        identity,
    )

    def turn(k, before):
        reached = k < here
        new = combine(before, jax.tree.map(lambda part: part[k], everything))
        return jax.tree.map(lambda a, b: jnp.where(reached, a, b), new, before)

    return lax.fori_loop(0, length, turn, start)


def column_shifts(values):
    zeros_col = jnp.zeros(values.shape[:-1] + (1,), values.dtype)
    left_view = jnp.concatenate([zeros_col, values[..., :-1]], axis=-1)
    right_view = jnp.concatenate([values[..., 1:], zeros_col], axis=-1)
    return (left_view, values, right_view)


def combine_pair(earlier, later):
    return (earlier[0] * later[0], later[0][:, None, None] * earlier[1] + later[1])


def on_device(frames_in, conv_weight, out_weight, skip_gain, decays):
    frame_total_count = frames_in.shape[0]
    channels = frames_in.shape[1]
    tile_rows = frames_in.shape[2]
    width = frames_in.shape[3]
    states = conv_weight.shape[2]
    cell_count = tile_rows * width
    padded = with_halo(frames_in, (("space", 2),), 1)
    column_views = column_shifts(padded)
    flat_views = [
        view.reshape(frame_total_count, channels, (tile_rows + 2) * width) for view in column_views
    ]
    frame_idx = 0
    accum = jnp.zeros((states, cell_count), jnp.float32)
    for vertical_shift in range(3):
        for col_off in range(3):
            window = flat_views[col_off][
                frame_idx, :, vertical_shift * width : vertical_shift * width + cell_count
            ]
            accum = accum + jnp.dot(
                conv_weight[vertical_shift, col_off], window, preferred_element_type=jnp.float32
            )
    frame_drives = [accum]
    driving = jnp.stack(frame_drives, axis=0).reshape(frame_total_count, states, tile_rows, width)
    in_gain = jnp.sqrt(1.0 - decays * decays)
    memory = jnp.zeros((states, tile_rows, width), jnp.float32)
    cumulative_damping = jnp.ones((states,), jnp.float32)
    frame_idx = 0
    memory = (
        decays[frame_idx][:, None, None] * memory
        + in_gain[frame_idx][:, None, None] * driving[frame_idx]
    )
    cumulative_damping = cumulative_damping * decays[frame_idx]
    local_states = [memory]
    decay_prods = [cumulative_damping]
    unit_decay = jnp.ones((states,), jnp.float32)
    propagated_state = entering(
        (cumulative_damping, memory), "tm", combine_pair, (unit_decay, jnp.zeros_like(memory))
    )[1]
    frame_idx = 0
    corrected = local_states[frame_idx] + decay_prods[frame_idx][:, None, None] * propagated_state
    rounded = corrected.astype(jnp.bfloat16).reshape(states, tile_rows * width)
    output = jnp.dot(out_weight, rounded, preferred_element_type=jnp.float32).reshape(
        channels, tile_rows, width
    )
    output = output + skip_gain[:, None, None] * frames_in[
        frame_idx, :, 0 : 0 + tile_rows, :
    ].astype(jnp.float32)
    results = [output.astype(jnp.bfloat16)]
    return jnp.stack(results, axis=0)


def solution(mesh):
    placed = (P("tm", None, "space", None), P(), P(), P(), P("tm", None))
    return jax.shard_map(
        on_device,
        mesh=mesh,
        in_specs=placed,
        out_specs=P("tm", None, "space", None),
        check_vma=False,
    )
```

profile of v0, /device:TPU:1, one launch (start us, length us, event | category | flops | bytes accessed | tf_op | source)
XLA Modules:
  0.0 638.1 jit_solution(3413738486186721323)
XLA Ops:
  41.9 28.0 %all-gather = f32[32,1,256]{2,1,0:T(1,128)S(1)} all-gather(f32[1,1,256]{2,1,0:T(1,128)S(1)} %bitcast.101), channel_id=1, replica_groups=mesh['tm'=32,'space'=4] {'tm'}, dimensions={0}, use_global_device_ids=true | all-gather | bytes 33792 | tf_op jit(solution)/shard_map/all_gather | solution.py:22
  75.4 346.2 %all-gather.3.cloned.1.call-done = f32[32,256,32,128]{3,2,1,0:T(8,128)} async-done(((f32[1,256,32,128]{3,2,1,0:T(8,128)}), f32[32,256,32,128]{3,2,1,0:T(8,128)}) %all-gather.3.cloned.1.call-update) | async-done | bytes 134217744 | tf_op jit(solution)/shard_map/all_gather | solution.py:22
  421.6 192.2 %while.14 = (s32[]{:T(128)}, f32[256,32,128]{2,1,0:T(8,128)}, s32[]{:T(128)}, f32[32,256]{1,0:T(8,128)S(1)}, f32[32,256,32,128]{3,2,1,0:T(8,128)}, /*index=5*/s32[]{:T(128)}, s32[]{:T(128)}) while((s32[]{:T(128)}, f32[256,32,128]{2,1,0:T(8,128)}, s32[]{:T(128)}, f32[32,256]{1,0:T(8,128)S(1)}, f32[32,256,32,128]{3,2,1,0:T(8,128)}, ...), condition=%wide.region_1.2_spmd.clone, body=%wide.region_0.1_spmd.clone.sunk | while | flops 4194308 | bytes 12586089 | solution.py:34
  426.3 6.0 fusion.27
  432.4 6.0 fusion.27
  438.4 6.0 fusion.27
  444.5 6.0 fusion.27
  450.5 6.0 fusion.27
  456.6 6.0 fusion.27
  462.6 6.0 fusion.27
  468.6 6.0 fusion.27
  474.7 6.0 fusion.27
  480.7 6.0 fusion.27
  486.8 6.0 fusion.27
  492.8 6.0 fusion.27
  498.9 6.0 fusion.27
  504.9 6.0 fusion.27
  511.0 6.0 fusion.27
  517.0 6.0 fusion.27
  523.1 6.0 fusion.27
  529.1 6.0 fusion.27
  535.1 6.0 fusion.27
  541.2 6.0 fusion.27
  547.2 6.0 fusion.27
  553.3 6.0 fusion.27
  559.3 6.0 fusion.27
  565.4 6.0 fusion.27
  571.4 6.0 fusion.27
  577.5 6.0 fusion.27
  583.5 6.0 fusion.27
  589.6 6.0 fusion.27
  595.6 6.0 fusion.27
  (77 shorter events, 75.2 us)
Async XLA Ops:
  6.5 611.3 %copy-start = (bf16[256,256]{1,0:T(8,128)(2,1)S(1)}, bf16[256,256]{1,0:T(8,128)(2,1)}, u32[]{:S(2)}) copy-start(bf16[256,256]{1,0:T(8,128)(2,1)} %param.9) | copy-start | bytes 393220
  6.5 8.3 %copy-start.3 = (f32[1,256]{1,0:T(1,128)S(1)}, f32[1,256]{1,0:T(1,128)}, u32[]{:S(2)}) copy-start(f32[1,256]{1,0:T(1,128)} %param.11) | copy-start | bytes 3076
  6.5 415.0 %all-gather.3.cloned.1.call-start = ((), (), s32[]{:S(2)}) async-start(), calls=%async_computation | async-start | bytes 138412032 | tf_op jit(solution)/shard_map/all_gather | solution.py:22
  9.6 5.3 collective-permute-start
  13.5 5.0 collective-permute-start.1
  21.8 1.3 copy-start.2
  621.5 5.7 copy-start.1
  621.5 5.7 copy-start.4
Sparse Core Ops, SparseCore 0:
  42.0 379.5 all-gather.2
where the time goes:
time: 639 us; the launch traced here: 638 us
  waiting for transfers between devices  350 us (55%)
  other arithmetic  205 us (32%)
  blocking collectives  28 us (4%)
  local copies, waits for them, and re-layouts  24 us (4%)
  between operations  13.6 us (2%)
  matrix products  12.5 us (2%)
    all_gather x1, waiting for transfers between devices, entering(): everything = jax.tree.map(lambda part: lax.all_gather(part, axis), array)  346 us
    select_n x32, other arithmetic, turn(): return jax.tree.map(lambda a, b: jnp.where(reached, a, b), new, before)  192 us
    all_gather x1, blocking collectives, entering(): everything = jax.tree.map(lambda part: lax.all_gather(part, axis), array)  28 us
  transfers between devices with their start and end apart: 3, of which 2 were waited for; matrix products, arithmetic and copies ran while one was open for 1% of the time, Pallas kernels for 0%

commit v1 on v0

v1 whole, which is shorter than its diff:
```python
import functools

import jax
import jax.numpy as jnp
from jax import lax
from jax.experimental import pallas as pl
from jax.experimental.pallas import tpu as pltpu
from jax.sharding import PartitionSpec as P

MESH = pl.DeviceIdType.MESH
ROWS = 32
HALF = 16
CH = 256
WIDTH = 128
CHIPS = 16
BAND = CH // CHIPS
CHUNKS = 4
STEP = HALF // CHUNKS
F32 = jnp.float32
BF16 = jnp.bfloat16


def column(row):
    return jnp.transpose(jnp.broadcast_to(row, (WIDTH, CH)), (1, 0))


def kernel(
    x_hbm, w_hbm, wo_hbm, skip_ref, dec_ref, y_hbm,
    xp, wc, wo, drive, coef, decs, achip, pair_out, pair_in, merged, up_in, down_out, entry,
    last_out, last_in, y_buf,
    load_sem, store_sem, halo_s, halo_r, dec_s, dec_r, a_s, a_r, pair_s, pair_r, up_s, up_r,
    down_s, down_r, last_s, last_r,
):
    tm = lax.axis_index("tm")
    sp = lax.axis_index("space")
    chip = tm // 2
    core = lax.rem(tm, 2)
    partner = chip * 2 + (1 - core)
    above = lax.rem(sp + 3, 4)
    below = lax.rem(sp + 1, 4)

    def peer(d):
        return lax.rem(chip + d, CHIPS)

    loads = [
        pltpu.make_async_copy(x_hbm, xp.at[pl.ds(1, ROWS)], load_sem.at[0]),
        pltpu.make_async_copy(wo_hbm, wo, load_sem.at[1]),
    ]
    for i in range(3):
        for j in range(3):
            loads.append(
                pltpu.make_async_copy(
                    w_hbm.at[i, j],
                    wc.at[pl.ds(j * CH, CH), pl.ds(i * CH, CH)],
                    load_sem.at[2 + 3 * i + j],
                )
            )
    for load in loads:
        load.start()

    barrier = pltpu.get_barrier_semaphore()

    def greet(d, carry):
        pl.semaphore_signal(
            barrier, inc=1, device_id={"tm": peer(d) * 2 + core}, device_id_type=MESH
        )
        return carry

    pl.semaphore_signal(barrier, inc=1, device_id={"tm": partner}, device_id_type=MESH)
    pl.semaphore_signal(barrier, inc=1, device_id={"space": above}, device_id_type=MESH)
    pl.semaphore_signal(barrier, inc=1, device_id={"space": below}, device_id_type=MESH)
    lax.fori_loop(1, CHIPS, greet, 0)

    own_decay = column(dec_ref[...])
    decs[0] = own_decay
    coef[0] = jnp.sqrt(1.0 - own_decay * own_decay)
    coef[4] = column(skip_ref[...])

    pl.semaphore_wait(barrier, CHIPS + 2)

    def halo(side):
        row, slot, target = ((ROWS - 1, 0, below), (0, ROWS + 1, above))[side]
        return pltpu.make_async_remote_copy(
            src_ref=x_hbm.at[row], dst_ref=xp.at[slot], send_sem=halo_s.at[side],
            recv_sem=halo_r.at[side], device_id={"space": target}, device_id_type=MESH,
        )

    halo(0).start()
    halo(1).start()
    dec_copy = pltpu.make_async_remote_copy(
        src_ref=decs.at[0], dst_ref=decs.at[1], send_sem=dec_s, recv_sem=dec_r,
        device_id={"tm": partner}, device_id_type=MESH,
    )
    dec_copy.start()
    for load in loads:
        load.wait()

    def first_row(s, q):
        return (1 - s) * (HALF - STEP * (q + 1)) + s * (STEP * q)

    lane = lax.broadcasted_iota(jnp.int32, (CH, WIDTH), 1)

    def conv_rows(h):
        view = [xp[h + i] for i in range(4)]
        right = jnp.concatenate(
            [jnp.concatenate([view[i], view[i + 1]], axis=1) for i in range(3)], axis=0
        )
        acc = jnp.dot(wc[...], right, preferred_element_type=F32)
        for e in range(2):
            part = acc[:, e * WIDTH : (e + 1) * WIDTH]
            left = jnp.where(lane == 0, 0.0, pltpu.roll(part[0:CH], 1, 1))
            after = jnp.where(lane == WIDTH - 1, 0.0, pltpu.roll(part[2 * CH :], WIDTH - 1, 1))
            drive[h + e] = coef[0] * (left + part[CH : 2 * CH] + after)

    def pair_copy(q):
        r = first_row(1 - core, q)
        return pltpu.make_async_remote_copy(
            src_ref=pair_out.at[pl.ds(r, STEP)], dst_ref=pair_in.at[pl.ds(r, STEP)],
            send_sem=pair_s.at[q], recv_sem=pair_r.at[q],
            device_id={"tm": partner}, device_id_type=MESH,
        )

    def pair_arrival(q):
        r = first_row(core, q)
        return pltpu.make_async_remote_copy(
            src_ref=pair_out.at[pl.ds(r, STEP)], dst_ref=pair_in.at[pl.ds(r, STEP)],
            send_sem=pair_s.at[q], recv_sem=pair_r.at[q],
            device_id={"tm": partner}, device_id_type=MESH,
        )

    def a_copy(d):
        to = peer(d)
        return pltpu.make_async_remote_copy(
            src_ref=coef.at[5, pl.ds(pl.multiple_of(to * BAND, BAND), BAND)],
            dst_ref=achip.at[chip],
            send_sem=a_s.at[d], recv_sem=a_r.at[d],
            device_id={"tm": to * 2 + core}, device_id_type=MESH,
        )

    def up_copy(q, d):
        to = peer(d)
        r = first_row(core, q)
        return pltpu.make_async_remote_copy(
            src_ref=merged.at[pl.ds(r, STEP), pl.ds(pl.multiple_of(to * BAND, BAND), BAND)],
            dst_ref=up_in.at[chip, pl.ds(r, STEP)],
            send_sem=up_s.at[q, d], recv_sem=up_r.at[q, d],
            device_id={"tm": to * 2 + core}, device_id_type=MESH,
        )

    def up_local(q):
        r = first_row(core, q)
        return pltpu.make_async_copy(
            merged.at[pl.ds(r, STEP), pl.ds(pl.multiple_of(chip * BAND, BAND), BAND)],
            up_in.at[chip, pl.ds(r, STEP)],
            up_s.at[q, 0],
        )

    def down_copy(q, d):
        to = peer(d)
        r = first_row(core, q)
        return pltpu.make_async_remote_copy(
            src_ref=down_out.at[to, pl.ds(r, STEP)],
            dst_ref=entry.at[pl.ds(r, STEP), pl.ds(pl.multiple_of(chip * BAND, BAND), BAND)],
            send_sem=down_s.at[q, d], recv_sem=down_r.at[q, d],
            device_id={"tm": to * 2 + core}, device_id_type=MESH,
        )

    def down_local(q):
        r = first_row(core, q)
        return pltpu.make_async_copy(
            down_out.at[chip, pl.ds(r, STEP)],
            entry.at[pl.ds(r, STEP), pl.ds(pl.multiple_of(chip * BAND, BAND), BAND)],
            down_s.at[q, 0],
        )

    def last_copy(q):
        r = first_row(core, q)
        return pltpu.make_async_remote_copy(
            src_ref=last_out.at[pl.ds(r, STEP)], dst_ref=last_in.at[pl.ds(r, STEP)],
            send_sem=last_s.at[q], recv_sem=last_r.at[q],
            device_id={"tm": partner}, device_id_type=MESH,
        )

    def last_arrival(q):
        r = first_row(1 - core, q)
        return pltpu.make_async_remote_copy(
            src_ref=last_out.at[pl.ds(r, STEP)], dst_ref=last_in.at[pl.ds(r, STEP)],
            send_sem=last_s.at[q], recv_sem=last_r.at[q],
            device_id={"tm": partner}, device_id_type=MESH,
        )

    def each(n0, n1, body):
        def run(i, carry):
            body(i)
            return carry

        lax.fori_loop(n0, n1, run, 0)

    other = 1 - core

    def send_half(q):
        @pl.when(q == CHUNKS - 1)
        def _():
            halo(0).wait()
            halo(1).wait()

            @pl.when(sp == 0)
            def _():
                xp[0] = jnp.zeros((CH, WIDTH), BF16)

            @pl.when(sp == 3)
            def _():
                xp[ROWS + 1] = jnp.zeros((CH, WIDTH), BF16)

        r0 = first_row(other, q)

        def tile(t):
            r = r0 + 2 * t
            conv_rows(r + HALF * other)
            for e in range(2):
                pair_out[r + e] = drive[r + HALF * other + e].astype(BF16)

        each(0, STEP // 2, tile)
        pair_copy(q).start()

    each(0, CHUNKS, send_half)

    dec_copy.wait()
    mine = decs[0]
    theirs = decs[1]
    second = core.astype(F32)
    coef[1] = (1.0 - second) * theirs + second
    coef[2] = (1.0 - second) + second * mine
    coef[5] = mine * theirs
    coef[3] = (1.0 - second) * mine + second * (mine * theirs)
    each(1, CHIPS, lambda d: a_copy(d).start())
    a_local = pltpu.make_async_copy(
        coef.at[5, pl.ds(pl.multiple_of(chip * BAND, BAND), BAND)], achip.at[chip], a_s.at[0]
    )
    a_local.start()

    def merge_half(q):
        r0 = first_row(core, q)

        def tile(t):
            conv_rows(r0 + 2 * t + HALF * core)

        each(0, STEP // 2, tile)
        pair_arrival(q).wait_recv()

        def merge(e):
            r = r0 + e
            own = drive[r + HALF * core]
            total = coef[1] * own + coef[2] * pair_in[r].astype(F32)
            merged[r] = total.astype(BF16)
            drive[r + HALF * core] = (1.0 - second) * own + second * total

        each(0, STEP, merge)
        each(1, CHIPS, lambda d: up_copy(q, d).start())
        up_local(q).start()

    each(0, CHUNKS, merge_half)

    each(1, CHIPS, lambda d: a_copy(d).wait())
    a_local.wait()

    def scan(q):
        each(1, CHIPS, lambda d: up_copy(q, d).wait_recv())
        up_local(q).wait()
        rows = pl.ds(first_row(core, q), STEP)
        state = jnp.zeros((STEP, BAND, WIDTH), F32)
        for i in range(CHIPS):
            down_out[i, rows] = state.astype(BF16)
            if i < CHIPS - 1:
                state = achip[i][None] * state + up_in[i, rows].astype(F32)
        each(1, CHIPS, lambda d: down_copy(q, d).start())
        down_local(q).start()

    each(0, CHUNKS, scan)

    def project(h, memory):
        out = jnp.dot(
            wo[...], jnp.concatenate(memory, axis=1), preferred_element_type=F32
        )
        for e in range(2):
            y_buf[h + e] = (
                out[:, e * WIDTH : (e + 1) * WIDTH] + coef[4] * xp[h + e + 1].astype(F32)
            ).astype(BF16)

    def y_copy(s, q, slot):
        h = first_row(s, q) + HALF * s
        return pltpu.make_async_copy(
            y_buf.at[pl.ds(h, STEP)], y_hbm.at[pl.ds(h, STEP)], store_sem.at[slot, q]
        )

    def finish(q):
        @pl.when(q < CHUNKS)
        def _():
            each(1, CHIPS, lambda d: down_copy(q, d).wait_recv())
            down_local(q).wait()
            r0 = first_row(core, q)

            def answer(e):
                r = r0 + e
                enter = entry[r].astype(F32)
                memory = coef[3] * enter + drive[r + HALF * core]
                drive[r + HALF * core] = memory
                last_out[r] = ((1.0 - second) * memory + second * enter).astype(BF16)

            each(0, STEP, answer)
            last_copy(q).start()

            def tile(t):
                h = r0 + 2 * t + HALF * core
                project(h, [drive[h + e].astype(BF16) for e in range(2)])

            each(0, STEP // 2, tile)
            y_copy(core, q, 0).start()

        @pl.when(q > 0)
        def _():
            p = q - 1
            last_arrival(p).wait_recv()
            r0 = first_row(other, p)

            def tile(t):
                r = r0 + 2 * t
                h = r + HALF * other
                project(
                    h,
                    [
                        (decs[0] * last_in[r + e].astype(F32) + drive[h + e]).astype(BF16)
                        for e in range(2)
                    ],
                )

            each(0, STEP // 2, tile)
            y_copy(other, p, 1).start()

    each(0, CHUNKS + 1, finish)

    def drain(q):
        pair_copy(q).wait_send()
        last_copy(q).wait_send()

        def one(d):
            up_copy(q, d).wait_send()
            down_copy(q, d).wait_send()

        each(1, CHIPS, one)
        y_copy(core, q, 0).wait()
        y_copy(other, q, 1).wait()

    each(0, CHUNKS, drain)


def on_device(frames_in, conv_weight, out_weight, skip_gain, decays):
    rows = jnp.transpose(frames_in[0], (1, 0, 2))
    dma = pltpu.SemaphoreType.DMA
    y = pl.pallas_call(
        kernel,
        out_shape=jax.ShapeDtypeStruct((ROWS, CH, WIDTH), BF16),
        in_specs=[
            pl.BlockSpec(memory_space=pl.ANY),
            pl.BlockSpec(memory_space=pl.ANY),
            pl.BlockSpec(memory_space=pl.ANY),
            pl.BlockSpec(memory_space=pltpu.VMEM),
            pl.BlockSpec(memory_space=pltpu.VMEM),
        ],
        out_specs=pl.BlockSpec(memory_space=pl.ANY),
        scratch_shapes=[
            pltpu.VMEM((ROWS + 2, CH, WIDTH), BF16),
            pltpu.VMEM((3 * CH, 3 * CH), BF16),
            pltpu.VMEM((CH, CH), BF16),
            pltpu.VMEM((ROWS, CH, WIDTH), F32),
            pltpu.VMEM((6, CH, WIDTH), F32),
            pltpu.VMEM((2, CH, WIDTH), F32),
            pltpu.VMEM((CHIPS, BAND, WIDTH), F32),
            pltpu.VMEM((HALF, CH, WIDTH), BF16),
            pltpu.VMEM((HALF, CH, WIDTH), BF16),
            pltpu.VMEM((HALF, CH, WIDTH), BF16),
            pltpu.VMEM((CHIPS, HALF, BAND, WIDTH), BF16),
            pltpu.VMEM((CHIPS, HALF, BAND, WIDTH), BF16),
            pltpu.VMEM((HALF, CH, WIDTH), BF16),
            pltpu.VMEM((HALF, CH, WIDTH), BF16),
            pltpu.VMEM((HALF, CH, WIDTH), BF16),
            pltpu.VMEM((ROWS, CH, WIDTH), BF16),
            dma((11,)),
            dma((2, CHUNKS)),
            dma((2,)),
            dma((2,)),
            dma,
            dma,
            dma((CHIPS,)),
            dma((CHIPS,)),
            dma((CHUNKS,)),
            dma((CHUNKS,)),
            dma((CHUNKS, CHIPS)),
            dma((CHUNKS, CHIPS)),
            dma((CHUNKS, CHIPS)),
            dma((CHUNKS, CHIPS)),
            dma((CHUNKS,)),
            dma((CHUNKS,)),
        ],
        compiler_params=pltpu.CompilerParams(
            collective_id=0, has_side_effects=True, vmem_limit_bytes=48 << 20
        ),
    )(rows, conv_weight, out_weight, skip_gain[None, :], decays)
    return jnp.transpose(y, (1, 0, 2))[None]


def solution(mesh):
    placed = (P("tm", None, "space", None), P(), P(), P(), P("tm", None))
    return jax.shard_map(
        on_device,
        mesh=mesh,
        in_specs=placed,
        out_specs=P("tm", None, "space", None),
        check_vma=False,
    )
```

time: 639 us -> 51.1 us (0.08)
  waiting for transfers between devices: 350 us -> 0 us
  other arithmetic: 205 us -> 0 us
  Pallas kernels: 0 us -> 45.8 us
  blocking collectives: 28 us -> 0 us
  local copies, waits for them, and re-layouts: 24 us -> 5.19 us
  between operations: 13.6 us -> 0.05 us
  matrix products: 12.5 us -> 0 us
    all_gather x1 -> x0, waiting for transfers between devices: 346 us -> none  [entering(): everything = jax.tree.map(lambda part: lax.all_gather(part, axis), array)]
    select_n x32 -> x0, other arithmetic: 192 us -> none  [turn(): return jax.tree.map(lambda a, b: jnp.where(reached, a, b), new, before)]
    pallas_call x0 -> x1, Pallas kernels: none -> 45.8 us  [on_device(): pl.pallas_call(kernel, out_shape=jax.ShapeDtypeStruct((ROWS, CH, WIDTH),...]
    all_gather x1 -> x0, blocking collectives: 28 us -> none  [entering(): everything = jax.tree.map(lambda part: lax.all_gather(part, axis), array)]
    dot_general x10 -> x0, matrix products: 12.5 us -> none  [the longest x9 8.86 us: on_device(): jnp.dot(conv_weight[vertical_shift, col_off], window, preferred_element_t...]
    another operation x2 -> x0, local copies, waits for them, and re-layouts: 11 us -> none  [on_device(): driving[frame_idx]]
    convert_element_type x2 -> x0, other arithmetic: 8.24 us -> none  [the longest x1 4.13 us: on_device(): results = [output.astype(jnp.bfloat16)]]
  transfers between devices with their start and end apart: 3 -> 0, of which waited for: 2 -> 0; matrix products, arithmetic and copies ran while one was open for 1% -> 0% of each run, Pallas kernels for 0% -> 0%
where the time goes in v1:
time: 51.1 us; the launch traced here: 51 us
  Pallas kernels  45.8 us (90%)
  local copies, waits for them, and re-layouts  5.19 us (10%)
    pallas_call x1, Pallas kernels, on_device(): pl.pallas_call(kernel, out_shape=jax.ShapeDtypeStruct((ROWS, CH, WIDTH),...  45.8 us
    broadcast_in_dim x1, local copies, waits for them, and re-layouts, on_device(): return jnp.transpose(y, (1, 0, 2))[None]  2.67 us
    unnamed x9, local copies, waits for them, and re-layouts  2.52 us

profile of v1, /device:TPU:1, one launch (start us, length us, event | category | flops | bytes accessed | tf_op | source)
XLA Modules:
  0.0 51.0 jit_solution(7542710865821835650)
XLA Ops:
  0.0 0.0 copy-start
  0.0 0.0 copy-start.1
  0.0 0.0 copy-start.2
  0.0 0.0 copy-start.3
  0.0 2.5 %copy.9 = bf16[1,256,32,128]{3,1,2,0:T(8,128)(2,1)S(1)} copy(bf16[1,256,32,128]{3,2,1,0:T(8,128)(2,1)} %param.5) | data formatting | bytes 4194304 | tf_op args[0]
  2.5 0.0 copy-done
  2.5 0.0 copy-done.1
  2.5 0.0 copy-done.2
  2.6 0.0 copy-done.3
  2.6 45.8 %shard_map.55 = bf16[32,256,128]{2,1,0:T(8,128)(2,1)S(1)} custom-call(bf16[32,256,128]{2,1,0:T(8,128)(2,1)S(1)} %bitcast.10, bf16[3,3,256,256]{3,2,1,0:T(8,128)(2,1)S(1)} %copy-done, bf16[256,256]{1,0:T(8,128)(2,1)S(1)} %copy-done.1, f32[1,256]{1,0:T(1,128)S(1)} %bitcast.11, f32[1,256]{1,0:T(1,128)S(1)} %copy-done.3), custom_call_target="tpu_custom_call" | custom-call | tf_op jit(solution)/shard_map/pallas_call | solution.py:360
  48.4 2.7 %copy.7 = bf16[1,256,32,128]{3,2,1,0:T(8,128)(2,1)} copy(bf16[1,256,32,128]{3,1,2,0:T(8,128)(2,1)S(1)} %bitcast.9) | data formatting | bytes 4194304 | tf_op jit(solution)/shard_map/broadcast_in_dim | solution.py:409
Async XLA Ops:
  0.0 2.5 %copy-start = (bf16[3,3,256,256]{3,2,1,0:T(8,128)(2,1)S(1)}, bf16[3,3,256,256]{3,2,1,0:T(8,128)(2,1)}, u32[]{:S(2)}) copy-start(bf16[3,3,256,256]{3,2,1,0:T(8,128)(2,1)} %w_hbm.1) | copy-start | bytes 3538948
  0.0 2.5 %copy-start.1 = (bf16[256,256]{1,0:T(8,128)(2,1)S(1)}, bf16[256,256]{1,0:T(8,128)(2,1)}, u32[]{:S(2)}) copy-start(bf16[256,256]{1,0:T(8,128)(2,1)} %wo_hbm.1) | copy-start | bytes 393220
  0.0 2.5 %copy-start.2 = (f32[256]{0:T(256)S(1)}, f32[256]{0:T(256)}, u32[]{:S(2)}) copy-start(f32[256]{0:T(256)} %param.8) | copy-start | bytes 3076
  0.0 2.5 %copy-start.3 = (f32[1,256]{1,0:T(1,128)S(1)}, f32[1,256]{1,0:T(1,128)}, u32[]{:S(2)}) copy-start(f32[1,256]{1,0:T(1,128)} %dec_ref.1) | copy-start | bytes 3076

commit v2 on v1

--- a/solution.py
+++ b/solution.py
@@ -15,6 +15,7 @@
 CHIPS = 16
 BAND = CH // CHIPS
 CHUNKS = 4
+LAG = 3
 STEP = HALF // CHUNKS
 F32 = jnp.float32
 BF16 = jnp.bfloat16
@@ -76,8 +77,6 @@
     coef[0] = jnp.sqrt(1.0 - own_decay * own_decay)
     coef[4] = column(skip_ref[...])
 
-    pl.semaphore_wait(barrier, CHIPS + 2)
-
     def halo(side):
         row, slot, target = ((ROWS - 1, 0, below), (0, ROWS + 1, above))[side]
         return pltpu.make_async_remote_copy(
@@ -85,32 +84,28 @@
             recv_sem=halo_r.at[side], device_id={"space": target}, device_id_type=MESH,
         )
 
-    halo(0).start()
-    halo(1).start()
     dec_copy = pltpu.make_async_remote_copy(
         src_ref=decs.at[0], dst_ref=decs.at[1], send_sem=dec_s, recv_sem=dec_r,
         device_id={"tm": partner}, device_id_type=MESH,
     )
-    dec_copy.start()
-    for load in loads:
-        load.wait()
 
     def first_row(s, q):
         return (1 - s) * (HALF - STEP * (q + 1)) + s * (STEP * q)
 
     lane = lax.broadcasted_iota(jnp.int32, (CH, WIDTH), 1)
 
-    def conv_rows(h):
+    def convolved(h):
         view = [xp[h + i] for i in range(4)]
         right = jnp.concatenate(
             [jnp.concatenate([view[i], view[i + 1]], axis=1) for i in range(3)], axis=0
         )
-        acc = jnp.dot(wc[...], right, preferred_element_type=F32)
-        for e in range(2):
-            part = acc[:, e * WIDTH : (e + 1) * WIDTH]
-            left = jnp.where(lane == 0, 0.0, pltpu.roll(part[0:CH], 1, 1))
-            after = jnp.where(lane == WIDTH - 1, 0.0, pltpu.roll(part[2 * CH :], WIDTH - 1, 1))
-            drive[h + e] = coef[0] * (left + part[CH : 2 * CH] + after)
+        return jnp.dot(wc[...], right, preferred_element_type=F32)
+
+    def driven(acc, e):
+        part = acc[:, e * WIDTH : (e + 1) * WIDTH]
+        left = jnp.where(lane == 0, 0.0, pltpu.roll(part[0:CH], 1, 1))
+        after = jnp.where(lane == WIDTH - 1, 0.0, pltpu.roll(part[2 * CH :], WIDTH - 1, 1))
+        return coef[0] * (left + part[CH : 2 * CH] + after)
 
     def pair_copy(q):
         r = first_row(1 - core, q)
@@ -197,56 +192,44 @@
         lax.fori_loop(n0, n1, run, 0)
 
     other = 1 - core
-
-    def send_half(q):
-        @pl.when(q == CHUNKS - 1)
-        def _():
-            halo(0).wait()
-            halo(1).wait()
-
-            @pl.when(sp == 0)
-            def _():
-                xp[0] = jnp.zeros((CH, WIDTH), BF16)
-
-            @pl.when(sp == 3)
-            def _():
-                xp[ROWS + 1] = jnp.zeros((CH, WIDTH), BF16)
-
+    second = core.astype(F32)
+
+    def conv(q):
         r0 = first_row(other, q)
+        r1 = first_row(core, q)
 
         def tile(t):
             r = r0 + 2 * t
-            conv_rows(r + HALF * other)
+            theirs = convolved(r + HALF * other)
+            h = r1 + 2 * t + HALF * core
+            ours = convolved(h)
             for e in range(2):
-                pair_out[r + e] = drive[r + HALF * other + e].astype(BF16)
+                value = driven(theirs, e)
+                drive[r + HALF * other + e] = value
+                pair_out[r + e] = value.astype(BF16)
+            for e in range(2):
+                drive[h + e] = driven(ours, e)
 
         each(0, STEP // 2, tile)
-        pair_copy(q).start()
-
-    each(0, CHUNKS, send_half)
-
-    dec_copy.wait()
-    mine = decs[0]
-    theirs = decs[1]
-    second = core.astype(F32)
-    coef[1] = (1.0 - second) * theirs + second
-    coef[2] = (1.0 - second) + second * mine
-    coef[5] = mine * theirs
-    coef[3] = (1.0 - second) * mine + second * (mine * theirs)
-    each(1, CHIPS, lambda d: a_copy(d).start())
+
     a_local = pltpu.make_async_copy(
         coef.at[5, pl.ds(pl.multiple_of(chip * BAND, BAND), BAND)], achip.at[chip], a_s.at[0]
     )
-    a_local.start()
+
+    def coefficients():
+        dec_copy.wait()
+        mine = decs[0]
+        theirs = decs[1]
+        coef[1] = (1.0 - second) * theirs + second
+        coef[2] = (1.0 - second) + second * mine
+        coef[5] = mine * theirs
+        coef[3] = (1.0 - second) * mine + second * (mine * theirs)
+        each(1, CHIPS, lambda d: a_copy(d).start())
+        a_local.start()
 
     def merge_half(q):
+        pair_arrival(q).wait_recv()
         r0 = first_row(core, q)
-
-        def tile(t):
-            conv_rows(r0 + 2 * t + HALF * core)
-
-        each(0, STEP // 2, tile)
-        pair_arrival(q).wait_recv()
 
         def merge(e):
             r = r0 + e
@@ -258,11 +241,6 @@
         each(0, STEP, merge)
         each(1, CHIPS, lambda d: up_copy(q, d).start())
         up_local(q).start()
-
-    each(0, CHUNKS, merge_half)
-
-    each(1, CHIPS, lambda d: a_copy(d).wait())
-    a_local.wait()
 
     def scan(q):
         each(1, CHIPS, lambda d: up_copy(q, d).wait_recv())
@@ -276,7 +254,52 @@
         each(1, CHIPS, lambda d: down_copy(q, d).start())
         down_local(q).start()
 
-    each(0, CHUNKS, scan)
+    for load in loads:
+        load.wait()
+    conv(0)
+    pl.semaphore_wait(barrier, CHIPS + 2)
+    halo(0).start()
+    halo(1).start()
+    dec_copy.start()
+    pair_copy(0).start()
+
+    def front(q):
+        @pl.when(q == CHUNKS - 1)
+        def _():
+            halo(0).wait()
+            halo(1).wait()
+
+            @pl.when(sp == 0)
+            def _():
+                xp[0] = jnp.zeros((CH, WIDTH), BF16)
+
+            @pl.when(sp == 3)
+            def _():
+                xp[ROWS + 1] = jnp.zeros((CH, WIDTH), BF16)
+
+        @pl.when(q < CHUNKS)
+        def _():
+            conv(q)
+            pair_copy(q).start()
+
+        @pl.when(q == 1)
+        def _():
+            coefficients()
+
+        @pl.when(q <= CHUNKS)
+        def _():
+            merge_half(q - 1)
+
+        @pl.when(q == LAG)
+        def _():
+            each(1, CHIPS, lambda d: a_copy(d).wait())
+            a_local.wait()
+
+        @pl.when(q >= LAG)
+        def _():
+            scan(q - LAG)
+
+    each(1, CHUNKS + LAG, front)
 
     def project(h, memory):
         out = jnp.dot(

time: 51.1 us -> 47.2 us (0.924)
  Pallas kernels: 45.8 us -> 41.9 us
    pallas_call x1, Pallas kernels: 45.8 us -> 41.9 us  [on_device(): pl.pallas_call(kernel, out_shape=jax.ShapeDtypeStruct((ROWS, CH, WIDTH),...]
where the time goes in v2:
time: 47.2 us; the launch traced here: 47.1 us
  Pallas kernels  41.9 us (89%)
  local copies, waits for them, and re-layouts  5.19 us (11%)
    pallas_call x1, Pallas kernels, on_device(): pl.pallas_call(kernel, out_shape=jax.ShapeDtypeStruct((ROWS, CH, WIDTH),...  41.9 us
    broadcast_in_dim x1, local copies, waits for them, and re-layouts, on_device(): return jnp.transpose(y, (1, 0, 2))[None]  2.67 us
    unnamed x9, local copies, waits for them, and re-layouts  2.52 us

profile of v2, /device:TPU:1, one launch (start us, length us, event | category | flops | bytes accessed | tf_op | source)
XLA Modules:
  0.0 47.1 jit_solution(13485674235961310599)
XLA Ops:
  0.0 0.0 copy-start
  0.0 0.0 copy-start.1
  0.0 0.0 copy-start.2
  0.0 0.0 copy-start.3
  0.0 2.5 %copy.9 = bf16[1,256,32,128]{3,1,2,0:T(8,128)(2,1)S(1)} copy(bf16[1,256,32,128]{3,2,1,0:T(8,128)(2,1)} %param.5) | data formatting | bytes 4194304 | tf_op args[0]
  2.5 0.0 copy-done
  2.5 0.0 copy-done.1
  2.5 0.0 copy-done.2
  2.6 0.0 copy-done.3
  2.6 41.9 %shard_map.55 = bf16[32,256,128]{2,1,0:T(8,128)(2,1)S(1)} custom-call(bf16[32,256,128]{2,1,0:T(8,128)(2,1)S(1)} %bitcast.10, bf16[3,3,256,256]{3,2,1,0:T(8,128)(2,1)S(1)} %copy-done, bf16[256,256]{1,0:T(8,128)(2,1)S(1)} %copy-done.1, f32[1,256]{1,0:T(1,128)S(1)} %bitcast.11, f32[1,256]{1,0:T(1,128)S(1)} %copy-done.3), custom_call_target="tpu_custom_call" | custom-call | tf_op jit(solution)/shard_map/pallas_call | solution.py:383
  44.4 2.7 %copy.7 = bf16[1,256,32,128]{3,2,1,0:T(8,128)(2,1)} copy(bf16[1,256,32,128]{3,1,2,0:T(8,128)(2,1)S(1)} %bitcast.9) | data formatting | bytes 4194304 | tf_op jit(solution)/shard_map/broadcast_in_dim | solution.py:432
Async XLA Ops:
  0.0 2.5 %copy-start = (bf16[3,3,256,256]{3,2,1,0:T(8,128)(2,1)S(1)}, bf16[3,3,256,256]{3,2,1,0:T(8,128)(2,1)}, u32[]{:S(2)}) copy-start(bf16[3,3,256,256]{3,2,1,0:T(8,128)(2,1)} %w_hbm.1) | copy-start | bytes 3538948
  0.0 2.5 %copy-start.1 = (bf16[256,256]{1,0:T(8,128)(2,1)S(1)}, bf16[256,256]{1,0:T(8,128)(2,1)}, u32[]{:S(2)}) copy-start(bf16[256,256]{1,0:T(8,128)(2,1)} %wo_hbm.1) | copy-start | bytes 393220
  0.0 2.5 %copy-start.2 = (f32[256]{0:T(256)S(1)}, f32[256]{0:T(256)}, u32[]{:S(2)}) copy-start(f32[256]{0:T(256)} %param.8) | copy-start | bytes 3076
  0.0 2.5 %copy-start.3 = (f32[1,256]{1,0:T(1,128)S(1)}, f32[1,256]{1,0:T(1,128)}, u32[]{:S(2)}) copy-start(f32[1,256]{1,0:T(1,128)} %dec_ref.1) | copy-start | bytes 3076

commit v3 on v2

--- a/solution.py
+++ b/solution.py
@@ -15,7 +15,10 @@
 CHIPS = 16
 BAND = CH // CHIPS
 CHUNKS = 4
-LAG = 3
+GROUP = 8
+EARLY = 0
+BLOCKS = 8
+VMEM_BYTES = 62 << 20
 STEP = HALF // CHUNKS
 F32 = jnp.float32
 BF16 = jnp.bfloat16
@@ -26,9 +29,9 @@
 
 
 def kernel(
-    x_hbm, w_hbm, wo_hbm, skip_ref, dec_ref, y_hbm,
+    x_hbm, w_hbm, wo_hbm, skip_hbm, dec_hbm, y_hbm,
     xp, wc, wo, drive, coef, decs, achip, pair_out, pair_in, merged, up_in, down_out, entry,
-    last_out, last_in, y_buf,
+    last_out, last_in, y_buf, y_rows, raw, stage, lines,
     load_sem, store_sem, halo_s, halo_r, dec_s, dec_r, a_s, a_r, pair_s, pair_r, up_s, up_r,
     down_s, down_r, last_s, last_r,
 ):
@@ -43,46 +46,73 @@
     def peer(d):
         return lax.rem(chip + d, CHIPS)
 
-    loads = [
-        pltpu.make_async_copy(x_hbm, xp.at[pl.ds(1, ROWS)], load_sem.at[0]),
-        pltpu.make_async_copy(wo_hbm, wo, load_sem.at[1]),
+    barrier = pltpu.get_barrier_semaphore()
+
+    def greet(d, carry):
+        pl.semaphore_signal(
+            barrier, inc=1, device_id={"tm": peer(d) * 2 + core}, device_id_type=MESH
+        )
+        return carry
+
+    pl.semaphore_signal(barrier, inc=1, device_id={"tm": partner}, device_id_type=MESH)
+    pl.semaphore_signal(barrier, inc=1, device_id={"space": above}, device_id_type=MESH)
+    pl.semaphore_signal(barrier, inc=1, device_id={"space": below}, device_id_type=MESH)
+    lax.fori_loop(1, CHIPS, greet, 0)
+
+    x_loads = [
+        pltpu.make_async_copy(
+            x_hbm.at[:, pl.ds(GROUP * b, GROUP)], raw.at[b], load_sem.at[b]
+        )
+        for b in range(ROWS // GROUP)
     ]
+    small_loads = [
+        pltpu.make_async_copy(dec_hbm, lines.at[0], load_sem.at[14]),
+        pltpu.make_async_copy(skip_hbm, lines.at[1], load_sem.at[15]),
+    ]
+    for load in small_loads:
+        load.start()
+    x_loads[1].start()
+    x_loads[2].start()
+    loads = []
     for i in range(3):
         for j in range(3):
             loads.append(
                 pltpu.make_async_copy(
                     w_hbm.at[i, j],
                     wc.at[pl.ds(j * CH, CH), pl.ds(i * CH, CH)],
-                    load_sem.at[2 + 3 * i + j],
+                    load_sem.at[5 + 3 * i + j],
                 )
             )
+    wo_load = pltpu.make_async_copy(wo_hbm, wo, load_sem.at[4])
     for load in loads:
         load.start()
-
-    barrier = pltpu.get_barrier_semaphore()
-
-    def greet(d, carry):
-        pl.semaphore_signal(
-            barrier, inc=1, device_id={"tm": peer(d) * 2 + core}, device_id_type=MESH
-        )
-        return carry
-
-    pl.semaphore_signal(barrier, inc=1, device_id={"tm": partner}, device_id_type=MESH)
-    pl.semaphore_signal(barrier, inc=1, device_id={"space": above}, device_id_type=MESH)
-    pl.semaphore_signal(barrier, inc=1, device_id={"space": below}, device_id_type=MESH)
-    lax.fori_loop(1, CHIPS, greet, 0)
-
-    own_decay = column(dec_ref[...])
+    x_loads[0].start()
+    x_loads[3].start()
+    wo_load.start()
+
+    for load in small_loads:
+        load.wait()
+    own_decay = column(lines[0])
     decs[0] = own_decay
     coef[0] = jnp.sqrt(1.0 - own_decay * own_decay)
-    coef[4] = column(skip_ref[...])
+    coef[4] = column(lines[1])
 
     def halo(side):
-        row, slot, target = ((ROWS - 1, 0, below), (0, ROWS + 1, above))[side]
-        return pltpu.make_async_remote_copy(
-            src_ref=x_hbm.at[row], dst_ref=xp.at[slot], send_sem=halo_s.at[side],
+        row, slot, target = ((ROWS, 0, below), (1, ROWS + 1, above))[side]
+        return pltpu.make_async_remote_copy(
+            src_ref=xp.at[row], dst_ref=xp.at[slot], send_sem=halo_s.at[side],
             recv_sem=halo_r.at[side], device_id={"space": target}, device_id_type=MESH,
         )
+
+    def reorder(b):
+        x_loads[b].wait()
+        stage[...] = raw[b].astype(F32).reshape(CH * GROUP, WIDTH)
+
+        def row(r):
+            xp[1 + GROUP * b + r] = stage[pl.ds(r, CH, stride=GROUP), :].astype(BF16)
+
+        for r in range(GROUP):
+            row(r)
 
     dec_copy = pltpu.make_async_remote_copy(
         src_ref=decs.at[0], dst_ref=decs.at[1], send_sem=dec_s, recv_sem=dec_r,
@@ -194,23 +224,17 @@
     other = 1 - core
     second = core.astype(F32)
 
-    def conv(q):
-        r0 = first_row(other, q)
-        r1 = first_row(core, q)
-
-        def tile(t):
-            r = r0 + 2 * t
-            theirs = convolved(r + HALF * other)
-            h = r1 + 2 * t + HALF * core
-            ours = convolved(h)
-            for e in range(2):
-                value = driven(theirs, e)
-                drive[r + HALF * other + e] = value
-                pair_out[r + e] = value.astype(BF16)
-            for e in range(2):
-                drive[h + e] = driven(ours, e)
-
-        each(0, STEP // 2, tile)
+    def conv_tile(q, t):
+        r = first_row(other, q) + 2 * t
+        theirs = convolved(r + HALF * other)
+        h = first_row(core, q) + 2 * t + HALF * core
+        ours = convolved(h)
+        for e in range(2):
+            value = driven(theirs, e)
+            drive[r + HALF * other + e] = value
+            pair_out[r + e] = value.astype(BF16)
+        for e in range(2):
+            drive[h + e] = driven(ours, e)
 
     a_local = pltpu.make_async_copy(
         coef.at[5, pl.ds(pl.multiple_of(chip * BAND, BAND), BAND)], achip.at[chip], a_s.at[0]
@@ -254,14 +278,19 @@
         each(1, CHIPS, lambda d: down_copy(q, d).start())
         down_local(q).start()
 
+    reorder(1)
+    reorder(2)
     for load in loads:
         load.wait()
-    conv(0)
+    each(0, STEP // 2, lambda t: conv_tile(0, t))
     pl.semaphore_wait(barrier, CHIPS + 2)
+    pair_copy(0).start()
+    dec_copy.start()
+    reorder(0)
+    reorder(3)
     halo(0).start()
     halo(1).start()
-    dec_copy.start()
-    pair_copy(0).start()
+    wo_load.wait()
 
     def front(q):
         @pl.when(q == CHUNKS - 1)
@@ -277,119 +306,132 @@
             def _():
                 xp[ROWS + 1] = jnp.zeros((CH, WIDTH), BF16)
 
-        @pl.when(q < CHUNKS)
-        def _():
-            conv(q)
-            pair_copy(q).start()
-
-        @pl.when(q == 1)
-        def _():
-            coefficients()
-
-        @pl.when(q <= CHUNKS)
+        def step(t):
+            conv_tile(q, t)
+
+            @pl.when((q == 1) & (t == 0))
+            def _():
+                coefficients()
+                merge_half(0)
+
+        each(0, STEP // 2, step)
+        pair_copy(q).start()
+
+        @pl.when(q > 1)
         def _():
             merge_half(q - 1)
 
-        @pl.when(q == LAG)
-        def _():
-            each(1, CHIPS, lambda d: a_copy(d).wait())
-            a_local.wait()
-
-        @pl.when(q >= LAG)
-        def _():
-            scan(q - LAG)
-
-    each(1, CHUNKS + LAG, front)
+    each(1, CHUNKS, front)
+    each(1, CHIPS, lambda d: a_copy(d).wait())
+    a_local.wait()
+    each(0, EARLY, scan)
+    merge_half(CHUNKS - 1)
+    each(EARLY, CHUNKS, scan)
 
     def project(h, memory):
         out = jnp.dot(
             wo[...], jnp.concatenate(memory, axis=1), preferred_element_type=F32
         )
         for e in range(2):
-            y_buf[h + e] = (
-                out[:, e * WIDTH : (e + 1) * WIDTH] + coef[4] * xp[h + e + 1].astype(F32)
-            ).astype(BF16)
+            row = h + e
+            y_rows[row // GROUP, pl.ds(lax.rem(row, GROUP), CH, stride=GROUP), :] = (
+                out[:, e * WIDTH : (e + 1) * WIDTH] + coef[4] * xp[row + 1].astype(F32)
+            )
 
     def y_copy(s, q, slot):
-        h = first_row(s, q) + HALF * s
+        b = (first_row(s, q) + HALF * s) // GROUP
         return pltpu.make_async_copy(
-            y_buf.at[pl.ds(h, STEP)], y_hbm.at[pl.ds(h, STEP)], store_sem.at[slot, q]
-        )
+            y_buf.at[b],
+            y_hbm.at[:, pl.ds(pl.multiple_of(b * GROUP, GROUP), GROUP)],
+            store_sem.at[slot, q],
+        )
+
+    def put(s, q, slot):
+        @pl.when(lax.rem(q, GROUP // STEP) == GROUP // STEP - 1)
+        def _():
+            b = (first_row(s, q) + HALF * s) // GROUP
+            y_buf[b] = y_rows[b].reshape(CH, GROUP, WIDTH).astype(BF16)
+            y_copy(s, q, slot).start()
 
     def finish(q):
-        @pl.when(q < CHUNKS)
+        pair_copy(q).wait_send()
+        each(1, CHIPS, lambda d: up_copy(q, d).wait_send())
+        each(1, CHIPS, lambda d: down_copy(q, d).wait_recv())
+        down_local(q).wait()
+        r0 = first_row(core, q)
+
+        def answer(e):
+            r = r0 + e
+            enter = entry[r].astype(F32)
+            memory = coef[3] * enter + drive[r + HALF * core]
+            drive[r + HALF * core] = memory
+            last_out[r] = ((1.0 - second) * memory + second * enter).astype(BF16)
+
+        each(0, STEP, answer)
+        last_copy(q).start()
+
+        def own_tile(t):
+            h = r0 + 2 * t + HALF * core
+            project(h, [drive[h + e].astype(BF16) for e in range(2)])
+
+        each(0, STEP // 2, own_tile)
+        put(core, q, 0)
+        last_arrival(q).wait_recv()
+        r1 = first_row(other, q)
+
+        def other_tile(t):
+            r = r1 + 2 * t
+            h = r + HALF * other
+            project(
+                h,
+                [
+                    (decs[0] * last_in[r + e].astype(F32) + drive[h + e]).astype(BF16)
+                    for e in range(2)
+                ],
+            )
+
+        each(0, STEP // 2, other_tile)
+        put(other, q, 1)
+        last_copy(q).wait_send()
+        each(1, CHIPS, lambda d: down_copy(q, d).wait_send())
+
+    each(0, CHUNKS, finish)
+
+    def drain(q):
+        @pl.when(lax.rem(q, GROUP // STEP) == GROUP // STEP - 1)
         def _():
-            each(1, CHIPS, lambda d: down_copy(q, d).wait_recv())
-            down_local(q).wait()
-            r0 = first_row(core, q)
-
-            def answer(e):
-                r = r0 + e
-                enter = entry[r].astype(F32)
-                memory = coef[3] * enter + drive[r + HALF * core]
-                drive[r + HALF * core] = memory
-                last_out[r] = ((1.0 - second) * memory + second * enter).astype(BF16)
-
-            each(0, STEP, answer)
-            last_copy(q).start()
-
-            def tile(t):
-                h = r0 + 2 * t + HALF * core
-                project(h, [drive[h + e].astype(BF16) for e in range(2)])
-
-            each(0, STEP // 2, tile)
-            y_copy(core, q, 0).start()
-
-        @pl.when(q > 0)
-        def _():
-            p = q - 1
-            last_arrival(p).wait_recv()
-            r0 = first_row(other, p)
-
-            def tile(t):
-                r = r0 + 2 * t
-                h = r + HALF * other
-                project(
-                    h,
-                    [
-                        (decs[0] * last_in[r + e].astype(F32) + drive[h + e]).astype(BF16)
-                        for e in range(2)
-                    ],
-                )
-
-            each(0, STEP // 2, tile)
-            y_copy(other, p, 1).start()
-
-    each(0, CHUNKS + 1, finish)
-
-    def drain(q):
-        pair_copy(q).wait_send()
-        last_copy(q).wait_send()
-
-        def one(d):
-            up_copy(q, d).wait_send()
-            down_copy(q, d).wait_send()
-
-        each(1, CHIPS, one)
-        y_copy(core, q, 0).wait()
-        y_copy(other, q, 1).wait()
+            y_copy(core, q, 0).wait()
+            y_copy(other, q, 1).wait()
 
     each(0, CHUNKS, drain)
 
 
+def settle(y_hbm, out_hbm, block, in_sem, out_sem):
+    part = CH // BLOCKS
+    fetch = [
+        pltpu.make_async_copy(y_hbm.at[pl.ds(part * b, part)], block.at[b], in_sem.at[b])
+        for b in range(BLOCKS)
+    ]
+    store = [
+        pltpu.make_async_copy(block.at[b], out_hbm.at[pl.ds(part * b, part)], out_sem.at[b])
+        for b in range(BLOCKS)
+    ]
+    for copy in fetch:
+        copy.start()
+    for b in range(BLOCKS):
+        fetch[b].wait()
+        store[b].start()
+    for copy in store:
+        copy.wait()
+
+
 def on_device(frames_in, conv_weight, out_weight, skip_gain, decays):
-    rows = jnp.transpose(frames_in[0], (1, 0, 2))
+    rows = frames_in[0]
     dma = pltpu.SemaphoreType.DMA
     y = pl.pallas_call(
         kernel,
-        out_shape=jax.ShapeDtypeStruct((ROWS, CH, WIDTH), BF16),
-        in_specs=[
-            pl.BlockSpec(memory_space=pl.ANY),
-            pl.BlockSpec(memory_space=pl.ANY),
-            pl.BlockSpec(memory_space=pl.ANY),
-            pl.BlockSpec(memory_space=pltpu.VMEM),
-            pl.BlockSpec(memory_space=pltpu.VMEM),
-        ],
+        out_shape=jax.ShapeDtypeStruct((CH, ROWS, WIDTH), BF16),
+        in_specs=[pl.BlockSpec(memory_space=pl.ANY)] * 5,
         out_specs=pl.BlockSpec(memory_space=pl.ANY),
         scratch_shapes=[
             pltpu.VMEM((ROWS + 2, CH, WIDTH), BF16),
@@ -407,8 +449,12 @@
             pltpu.VMEM((HALF, CH, WIDTH), BF16),
             pltpu.VMEM((HALF, CH, WIDTH), BF16),
             pltpu.VMEM((HALF, CH, WIDTH), BF16),
-            pltpu.VMEM((ROWS, CH, WIDTH), BF16),
-            dma((11,)),
+            pltpu.VMEM((ROWS // GROUP, CH, GROUP, WIDTH), BF16),
+            pltpu.VMEM((ROWS // GROUP, CH * GROUP, WIDTH), F32),
+            pltpu.VMEM((ROWS // GROUP, CH, GROUP, WIDTH), BF16),
+            pltpu.VMEM((CH * GROUP, WIDTH), F32),
+            pltpu.VMEM((2, 1, CH), F32),
+            dma((16,)),
             dma((2, CHUNKS)),
             dma((2,)),
             dma((2,)),
@@ -426,10 +472,22 @@
             dma((CHUNKS,)),
         ],
         compiler_params=pltpu.CompilerParams(
-            collective_id=0, has_side_effects=True, vmem_limit_bytes=48 << 20
+            collective_id=0, has_side_effects=True, vmem_limit_bytes=VMEM_BYTES
         ),
     )(rows, conv_weight, out_weight, skip_gain[None, :], decays)
-    return jnp.transpose(y, (1, 0, 2))[None]
+    settled = pl.pallas_call(
+        settle,
+        out_shape=jax.ShapeDtypeStruct((CH, ROWS, WIDTH), BF16),
+        in_specs=[pl.BlockSpec(memory_space=pl.ANY)],
+        out_specs=pl.BlockSpec(memory_space=pl.ANY),
+        scratch_shapes=[
+            pltpu.VMEM((BLOCKS, CH // BLOCKS, ROWS, WIDTH), BF16),
+            dma((BLOCKS,)),
+            dma((BLOCKS,)),
+        ],
+        compiler_params=pltpu.CompilerParams(vmem_limit_bytes=VMEM_BYTES),
+    )(y)
+    return settled[None]
 
 
 def solution(mesh):

time: 47.2 us -> 45.1 us (0.956)
  local copies, waits for them, and re-layouts: 5.19 us -> 0 us
  Pallas kernels: 41.9 us -> 45 us
    pallas_call x1 -> x2, Pallas kernels: 41.9 us -> 45 us  [the longest x1 42.6 us: on_device(): pl.pallas_call(kernel, out_shape=jax.ShapeDtypeStruct((CH, ROWS, WIDTH),...]
    broadcast_in_dim x1 -> x0, local copies, waits for them, and re-layouts: 2.67 us -> none  [on_device(): return jnp.transpose(y, (1, 0, 2))[None]]
    unnamed x9 -> x0, local copies, waits for them, and re-layouts: 2.52 us -> none
where the time goes in v3:
time: 45.1 us; the launch traced here: 45 us
  Pallas kernels  45 us (100%)
    pallas_call x1, Pallas kernels, on_device(): pl.pallas_call(kernel, out_shape=jax.ShapeDtypeStruct((CH, ROWS, WIDTH),...  42.6 us
    pallas_call x1, Pallas kernels, on_device(): pl.pallas_call(settle, out_shape=jax.ShapeDtypeStruct((CH, ROWS, WIDTH),...  2.39 us

profile of v3, /device:TPU:1, one launch (start us, length us, event | category | flops | bytes accessed | tf_op | source)
XLA Modules:
  0.0 45.0 jit_solution(14072502722636356520)
XLA Ops:
  0.0 42.6 %shard_map.55.y_hbm = bf16[256,32,128]{2,1,0:T(8,128)(2,1)} custom-call(bf16[256,32,128]{2,1,0:T(8,128)(2,1)} %bitcast.3, bf16[3,3,256,256]{3,2,1,0:T(8,128)(2,1)} %w_hbm.1, bf16[256,256]{1,0:T(8,128)(2,1)} %wo_hbm.1, f32[1,256]{1,0:T(1,128)} %bitcast.4, f32[1,256]{1,0:T(1,128)} %dec_hbm.1), custom_call_target="tpu_custom_call" | custom-call | tf_op jit(solution)/shard_map/pallas_call | solution.py:431
  42.6 2.4 %shard_map.56 = bf16[256,32,128]{2,1,0:T(8,128)(2,1)} custom-call(bf16[256,32,128]{2,1,0:T(8,128)(2,1)} %shard_map.55.y_hbm), custom_call_target="tpu_custom_call" | custom-call | tf_op jit(solution)/shard_map/pallas_call | solution.py:478

commit v4 on v3

--- a/solution.py
+++ b/solution.py
@@ -17,8 +17,7 @@
 CHUNKS = 4
 GROUP = 8
 EARLY = 0
-BLOCKS = 8
-VMEM_BYTES = 62 << 20
+VMEM_BYTES = 48 << 20
 STEP = HALF // CHUNKS
 F32 = jnp.float32
 BF16 = jnp.bfloat16
@@ -29,10 +28,10 @@
 
 
 def kernel(
-    x_hbm, w_hbm, wo_hbm, skip_hbm, dec_hbm, y_hbm,
+    x_hbm, w_hbm, wo_hbm, skip_hbm, dec_hbm, y_out,
     xp, wc, wo, drive, coef, decs, achip, pair_out, pair_in, merged, up_in, down_out, entry,
-    last_out, last_in, y_buf, y_rows, raw, stage, lines,
-    load_sem, store_sem, halo_s, halo_r, dec_s, dec_r, a_s, a_r, pair_s, pair_r, up_s, up_r,
+    last_out, last_in, y_rows, raw, stage, lines,
+    load_sem, halo_s, halo_r, dec_s, dec_r, a_s, a_r, pair_s, pair_r, up_s, up_r,
     down_s, down_r, last_s, last_r,
 ):
     tm = lax.axis_index("tm")
@@ -115,7 +114,7 @@
             row(r)
 
     dec_copy = pltpu.make_async_remote_copy(
-        src_ref=decs.at[0], dst_ref=decs.at[1], send_sem=dec_s, recv_sem=dec_r,
+        src_ref=lines.at[0], dst_ref=lines.at[2], send_sem=dec_s, recv_sem=dec_r,
         device_id={"tm": partner}, device_id_type=MESH,
     )
 
@@ -243,7 +242,7 @@
     def coefficients():
         dec_copy.wait()
         mine = decs[0]
-        theirs = decs[1]
+        theirs = column(lines[2])
         coef[1] = (1.0 - second) * theirs + second
         coef[2] = (1.0 - second) + second * mine
         coef[5] = mine * theirs
@@ -283,14 +282,14 @@
     for load in loads:
         load.wait()
     each(0, STEP // 2, lambda t: conv_tile(0, t))
-    pl.semaphore_wait(barrier, CHIPS + 2)
-    pair_copy(0).start()
-    dec_copy.start()
     reorder(0)
     reorder(3)
+    wo_load.wait()
+    pl.semaphore_wait(barrier, CHIPS + 2)
+    dec_copy.start()
+    pair_copy(0).start()
     halo(0).start()
     halo(1).start()
-    wo_load.wait()
 
     def front(q):
         @pl.when(q == CHUNKS - 1)
@@ -338,20 +337,13 @@
                 out[:, e * WIDTH : (e + 1) * WIDTH] + coef[4] * xp[row + 1].astype(F32)
             )
 
-    def y_copy(s, q, slot):
-        b = (first_row(s, q) + HALF * s) // GROUP
-        return pltpu.make_async_copy(
-            y_buf.at[b],
-            y_hbm.at[:, pl.ds(pl.multiple_of(b * GROUP, GROUP), GROUP)],
-            store_sem.at[slot, q],
-        )
-
-    def put(s, q, slot):
+    def put(s, q):
         @pl.when(lax.rem(q, GROUP // STEP) == GROUP // STEP - 1)
         def _():
             b = (first_row(s, q) + HALF * s) // GROUP
-            y_buf[b] = y_rows[b].reshape(CH, GROUP, WIDTH).astype(BF16)
-            y_copy(s, q, slot).start()
+            y_out[:, pl.ds(pl.multiple_of(b * GROUP, GROUP), GROUP)] = (
+                y_rows[b].reshape(CH, GROUP, WIDTH).astype(BF16)
+            )
 
     def finish(q):
         pair_copy(q).wait_send()
@@ -375,7 +367,7 @@
             project(h, [drive[h + e].astype(BF16) for e in range(2)])
 
         each(0, STEP // 2, own_tile)
-        put(core, q, 0)
+        put(core, q)
         last_arrival(q).wait_recv()
         r1 = first_row(other, q)
 
@@ -391,55 +383,29 @@
             )
 
         each(0, STEP // 2, other_tile)
-        put(other, q, 1)
+        put(other, q)
         last_copy(q).wait_send()
         each(1, CHIPS, lambda d: down_copy(q, d).wait_send())
 
     each(0, CHUNKS, finish)
 
-    def drain(q):
-        @pl.when(lax.rem(q, GROUP // STEP) == GROUP // STEP - 1)
-        def _():
-            y_copy(core, q, 0).wait()
-            y_copy(other, q, 1).wait()
-
-    each(0, CHUNKS, drain)
-
-
-def settle(y_hbm, out_hbm, block, in_sem, out_sem):
-    part = CH // BLOCKS
-    fetch = [
-        pltpu.make_async_copy(y_hbm.at[pl.ds(part * b, part)], block.at[b], in_sem.at[b])
-        for b in range(BLOCKS)
-    ]
-    store = [
-        pltpu.make_async_copy(block.at[b], out_hbm.at[pl.ds(part * b, part)], out_sem.at[b])
-        for b in range(BLOCKS)
-    ]
-    for copy in fetch:
-        copy.start()
-    for b in range(BLOCKS):
-        fetch[b].wait()
-        store[b].start()
-    for copy in store:
-        copy.wait()
-
 
 def on_device(frames_in, conv_weight, out_weight, skip_gain, decays):
     rows = frames_in[0]
+    pin = lambda a: pltpu.with_memory_space_constraint(a, pltpu.HBM)
     dma = pltpu.SemaphoreType.DMA
     y = pl.pallas_call(
         kernel,
         out_shape=jax.ShapeDtypeStruct((CH, ROWS, WIDTH), BF16),
         in_specs=[pl.BlockSpec(memory_space=pl.ANY)] * 5,
-        out_specs=pl.BlockSpec(memory_space=pl.ANY),
+        out_specs=pl.BlockSpec(memory_space=pltpu.VMEM),
         scratch_shapes=[
             pltpu.VMEM((ROWS + 2, CH, WIDTH), BF16),
             pltpu.VMEM((3 * CH, 3 * CH), BF16),
             pltpu.VMEM((CH, CH), BF16),
             pltpu.VMEM((ROWS, CH, WIDTH), F32),
             pltpu.VMEM((6, CH, WIDTH), F32),
-            pltpu.VMEM((2, CH, WIDTH), F32),
+            pltpu.VMEM((1, CH, WIDTH), F32),
             pltpu.VMEM((CHIPS, BAND, WIDTH), F32),
             pltpu.VMEM((HALF, CH, WIDTH), BF16),
             pltpu.VMEM((HALF, CH, WIDTH), BF16),
@@ -449,13 +415,11 @@
             pltpu.VMEM((HALF, CH, WIDTH), BF16),
             pltpu.VMEM((HALF, CH, WIDTH), BF16),
             pltpu.VMEM((HALF, CH, WIDTH), BF16),
-            pltpu.VMEM((ROWS // GROUP, CH, GROUP, WIDTH), BF16),
             pltpu.VMEM((ROWS // GROUP, CH * GROUP, WIDTH), F32),
             pltpu.VMEM((ROWS // GROUP, CH, GROUP, WIDTH), BF16),
             pltpu.VMEM((CH * GROUP, WIDTH), F32),
-            pltpu.VMEM((2, 1, CH), F32),
+            pltpu.VMEM((3, 1, CH), F32),
             dma((16,)),
-            dma((2, CHUNKS)),
             dma((2,)),
             dma((2,)),
             dma,
@@ -474,20 +438,8 @@
         compiler_params=pltpu.CompilerParams(
             collective_id=0, has_side_effects=True, vmem_limit_bytes=VMEM_BYTES
         ),
-    )(rows, conv_weight, out_weight, skip_gain[None, :], decays)
-    settled = pl.pallas_call(
-        settle,
-        out_shape=jax.ShapeDtypeStruct((CH, ROWS, WIDTH), BF16),
-        in_specs=[pl.BlockSpec(memory_space=pl.ANY)],
-        out_specs=pl.BlockSpec(memory_space=pl.ANY),
-        scratch_shapes=[
-            pltpu.VMEM((BLOCKS, CH // BLOCKS, ROWS, WIDTH), BF16),
-            dma((BLOCKS,)),
-            dma((BLOCKS,)),
-        ],
-        compiler_params=pltpu.CompilerParams(vmem_limit_bytes=VMEM_BYTES),
-    )(y)
-    return settled[None]
+    )(pin(rows), pin(conv_weight), pin(out_weight), pin(skip_gain[None, :]), pin(decays))
+    return y[None]
 
 
 def solution(mesh):

time: 45.1 us -> 43.3 us (0.960)
  Pallas kernels: 45 us -> 41.9 us
  local copies, waits for them, and re-layouts: 0 us -> 1.32 us
    pallas_call x1 -> x0, Pallas kernels: 2.39 us -> none  [on_device(): pl.pallas_call(settle, out_shape=jax.ShapeDtypeStruct((CH, ROWS, WIDTH),...]
    unnamed x0 -> x1, local copies, waits for them, and re-layouts: none -> 1.32 us
    pallas_call x1, Pallas kernels: 42.6 us -> 41.9 us  [on_device(): pl.pallas_call(kernel, out_shape=jax.ShapeDtypeStruct((CH, ROWS, WIDTH),...]
where the time goes in v4:
time: 43.3 us; the launch traced here: 43.2 us
  Pallas kernels  41.9 us (97%)
  local copies, waits for them, and re-layouts  1.32 us (3%)
    pallas_call x1, Pallas kernels, on_device(): pl.pallas_call(kernel, out_shape=jax.ShapeDtypeStruct((CH, ROWS, WIDTH),...  41.9 us
    unnamed x1, local copies, waits for them, and re-layouts  1.32 us

profile of v4, /device:TPU:1, one launch (start us, length us, event | category | flops | bytes accessed | tf_op | source)
XLA Modules:
  0.0 43.2 jit_solution(15338178125944953452)
XLA Ops:
  0.0 41.9 %shard_map.55 = bf16[256,32,128]{2,1,0:T(8,128)(2,1)S(1)} custom-call(bf16[256,32,128]{2,1,0:T(8,128)(2,1)} %bitcast.4, bf16[3,3,256,256]{3,2,1,0:T(8,128)(2,1)} %w_hbm.1, bf16[256,256]{1,0:T(8,128)(2,1)} %wo_hbm.1, f32[1,256]{1,0:T(1,128)} %bitcast.5, f32[1,256]{1,0:T(1,128)} %dec_hbm.1), custom_call_target="tpu_custom_call" | custom-call | tf_op jit(solution)/shard_map/pallas_call | solution.py:397
  41.9 1.3 %copy.7 = bf16[1,256,32,128]{3,2,1,0:T(8,128)(2,1)} copy(bf16[1,256,32,128]{3,2,1,0:T(8,128)(2,1)S(1)} %bitcast.3) | data formatting | bytes 4194304

commit v5 on v4

--- a/solution.py
+++ b/solution.py
@@ -32,7 +32,7 @@
     xp, wc, wo, drive, coef, decs, achip, pair_out, pair_in, merged, up_in, down_out, entry,
     last_out, last_in, y_rows, raw, stage, lines,
     load_sem, halo_s, halo_r, dec_s, dec_r, a_s, a_r, pair_s, pair_r, up_s, up_r,
-    down_s, down_r, last_s, last_r,
+    down_s, down_r, last_s, last_r, near_a, near_up, near_down,
 ):
     tm = lax.axis_index("tm")
     sp = lax.axis_index("space")
@@ -65,8 +65,8 @@
         for b in range(ROWS // GROUP)
     ]
     small_loads = [
-        pltpu.make_async_copy(dec_hbm, lines.at[0], load_sem.at[14]),
-        pltpu.make_async_copy(skip_hbm, lines.at[1], load_sem.at[15]),
+        pltpu.make_async_copy(dec_hbm, lines.at[0], load_sem.at[6]),
+        pltpu.make_async_copy(skip_hbm, lines.at[1], load_sem.at[7]),
     ]
     for load in small_loads:
         load.start()
@@ -79,7 +79,7 @@
                 pltpu.make_async_copy(
                     w_hbm.at[i, j],
                     wc.at[pl.ds(j * CH, CH), pl.ds(i * CH, CH)],
-                    load_sem.at[5 + 3 * i + j],
+                    load_sem.at[5],
                 )
             )
     wo_load = pltpu.make_async_copy(wo_hbm, wo, load_sem.at[4])
@@ -157,7 +157,7 @@
         return pltpu.make_async_remote_copy(
             src_ref=coef.at[5, pl.ds(pl.multiple_of(to * BAND, BAND), BAND)],
             dst_ref=achip.at[chip],
-            send_sem=a_s.at[d], recv_sem=a_r.at[d],
+            send_sem=a_s, recv_sem=a_r,
             device_id={"tm": to * 2 + core}, device_id_type=MESH,
         )
 
@@ -167,7 +167,7 @@
         return pltpu.make_async_remote_copy(
             src_ref=merged.at[pl.ds(r, STEP), pl.ds(pl.multiple_of(to * BAND, BAND), BAND)],
             dst_ref=up_in.at[chip, pl.ds(r, STEP)],
-            send_sem=up_s.at[q, d], recv_sem=up_r.at[q, d],
+            send_sem=up_s.at[q], recv_sem=up_r.at[q],
             device_id={"tm": to * 2 + core}, device_id_type=MESH,
         )
 
@@ -176,7 +176,7 @@
         return pltpu.make_async_copy(
             merged.at[pl.ds(r, STEP), pl.ds(pl.multiple_of(chip * BAND, BAND), BAND)],
             up_in.at[chip, pl.ds(r, STEP)],
-            up_s.at[q, 0],
+            near_up.at[q],
         )
 
     def down_copy(q, d):
@@ -185,7 +185,7 @@
         return pltpu.make_async_remote_copy(
             src_ref=down_out.at[to, pl.ds(r, STEP)],
             dst_ref=entry.at[pl.ds(r, STEP), pl.ds(pl.multiple_of(chip * BAND, BAND), BAND)],
-            send_sem=down_s.at[q, d], recv_sem=down_r.at[q, d],
+            send_sem=down_s.at[q], recv_sem=down_r.at[q],
             device_id={"tm": to * 2 + core}, device_id_type=MESH,
         )
 
@@ -194,7 +194,7 @@
         return pltpu.make_async_copy(
             down_out.at[chip, pl.ds(r, STEP)],
             entry.at[pl.ds(r, STEP), pl.ds(pl.multiple_of(chip * BAND, BAND), BAND)],
-            down_s.at[q, 0],
+            near_down.at[q],
         )
 
     def last_copy(q):
@@ -210,6 +210,27 @@
         return pltpu.make_async_remote_copy(
             src_ref=last_out.at[pl.ds(r, STEP)], dst_ref=last_in.at[pl.ds(r, STEP)],
             send_sem=last_s.at[q], recv_sem=last_r.at[q],
+            device_id={"tm": partner}, device_id_type=MESH,
+        )
+
+    def a_all():
+        part = achip.at[pl.ds(0, CHIPS - 1)]
+        return pltpu.make_async_remote_copy(
+            src_ref=part, dst_ref=part, send_sem=a_s, recv_sem=a_r,
+            device_id={"tm": partner}, device_id_type=MESH,
+        )
+
+    def up_all(q):
+        part = up_in.at[pl.ds(0, CHIPS - 1), pl.ds(first_row(core, q), STEP)]
+        return pltpu.make_async_remote_copy(
+            src_ref=part, dst_ref=part, send_sem=up_s.at[q], recv_sem=up_r.at[q],
+            device_id={"tm": partner}, device_id_type=MESH,
+        )
+
+    def down_all(q):
+        part = down_out.at[pl.ds(0, CHIPS - 1), pl.ds(first_row(core, q), STEP)]
+        return pltpu.make_async_remote_copy(
+            src_ref=part, dst_ref=part, send_sem=down_s.at[q], recv_sem=down_r.at[q],
             device_id={"tm": partner}, device_id_type=MESH,
         )
 
@@ -236,7 +257,7 @@
             drive[h + e] = driven(ours, e)
 
     a_local = pltpu.make_async_copy(
-        coef.at[5, pl.ds(pl.multiple_of(chip * BAND, BAND), BAND)], achip.at[chip], a_s.at[0]
+        coef.at[5, pl.ds(pl.multiple_of(chip * BAND, BAND), BAND)], achip.at[chip], near_a
     )
 
     def coefficients():
@@ -247,8 +268,6 @@
         coef[2] = (1.0 - second) + second * mine
         coef[5] = mine * theirs
         coef[3] = (1.0 - second) * mine + second * (mine * theirs)
-        each(1, CHIPS, lambda d: a_copy(d).start())
-        a_local.start()
 
     def merge_half(q):
         pair_arrival(q).wait_recv()
@@ -266,7 +285,7 @@
         up_local(q).start()
 
     def scan(q):
-        each(1, CHIPS, lambda d: up_copy(q, d).wait_recv())
+        up_all(q).wait_recv()
         up_local(q).wait()
         rows = pl.ds(first_row(core, q), STEP)
         state = jnp.zeros((STEP, BAND, WIDTH), F32)
@@ -279,8 +298,7 @@
 
     reorder(1)
     reorder(2)
-    for load in loads:
-        load.wait()
+    pltpu.make_async_copy(wc, wc, load_sem.at[5]).wait()
     each(0, STEP // 2, lambda t: conv_tile(0, t))
     reorder(0)
     reorder(3)
@@ -312,6 +330,8 @@
             def _():
                 coefficients()
                 merge_half(0)
+                each(1, CHIPS, lambda d: a_copy(d).start())
+                a_local.start()
 
         each(0, STEP // 2, step)
         pair_copy(q).start()
@@ -321,7 +341,7 @@
             merge_half(q - 1)
 
     each(1, CHUNKS, front)
-    each(1, CHIPS, lambda d: a_copy(d).wait())
+    a_all().wait()
     a_local.wait()
     each(0, EARLY, scan)
     merge_half(CHUNKS - 1)
@@ -347,8 +367,8 @@
 
     def finish(q):
         pair_copy(q).wait_send()
-        each(1, CHIPS, lambda d: up_copy(q, d).wait_send())
-        each(1, CHIPS, lambda d: down_copy(q, d).wait_recv())
+        up_all(q).wait_send()
+        down_all(q).wait_recv()
         down_local(q).wait()
         r0 = first_row(core, q)
 
@@ -385,7 +405,7 @@
         each(0, STEP // 2, other_tile)
         put(other, q)
         last_copy(q).wait_send()
-        each(1, CHIPS, lambda d: down_copy(q, d).wait_send())
+        down_all(q).wait_send()
 
     each(0, CHUNKS, finish)
 
@@ -419,19 +439,22 @@
             pltpu.VMEM((ROWS // GROUP, CH, GROUP, WIDTH), BF16),
             pltpu.VMEM((CH * GROUP, WIDTH), F32),
             pltpu.VMEM((3, 1, CH), F32),
-            dma((16,)),
+            dma((8,)),
             dma((2,)),
             dma((2,)),
             dma,
             dma,
-            dma((CHIPS,)),
-            dma((CHIPS,)),
-            dma((CHUNKS,)),
-            dma((CHUNKS,)),
-            dma((CHUNKS, CHIPS)),
-            dma((CHUNKS, CHIPS)),
-            dma((CHUNKS, CHIPS)),
-            dma((CHUNKS, CHIPS)),
+            dma,
+            dma,
+            dma((CHUNKS,)),
+            dma((CHUNKS,)),
+            dma((CHUNKS,)),
+            dma((CHUNKS,)),
+            dma((CHUNKS,)),
+            dma((CHUNKS,)),
+            dma((CHUNKS,)),
+            dma((CHUNKS,)),
+            dma,
             dma((CHUNKS,)),
             dma((CHUNKS,)),
         ],

time: 43.3 us -> 41 us (0.947)
  Pallas kernels: 41.9 us -> 39.5 us
    pallas_call x1, Pallas kernels: 41.9 us -> 39.5 us  [on_device(): pl.pallas_call(kernel, out_shape=jax.ShapeDtypeStruct((CH, ROWS, WIDTH),...]
where the time goes in v5:
time: 41 us; the launch traced here: 40.9 us
  Pallas kernels  39.5 us (96%)
  local copies, waits for them, and re-layouts  1.32 us (3%)
    pallas_call x1, Pallas kernels, on_device(): pl.pallas_call(kernel, out_shape=jax.ShapeDtypeStruct((CH, ROWS, WIDTH),...  39.5 us
    unnamed x1, local copies, waits for them, and re-layouts  1.32 us

profile of v5, /device:TPU:1, one launch (start us, length us, event | category | flops | bytes accessed | tf_op | source)
XLA Modules:
  0.0 40.9 jit_solution(12733005719174393845)
XLA Ops:
  0.0 39.5 %shard_map.55 = bf16[256,32,128]{2,1,0:T(8,128)(2,1)S(1)} custom-call(bf16[256,32,128]{2,1,0:T(8,128)(2,1)} %bitcast.4, bf16[3,3,256,256]{3,2,1,0:T(8,128)(2,1)} %w_hbm.1, bf16[256,256]{1,0:T(8,128)(2,1)} %wo_hbm.1, f32[1,256]{1,0:T(1,128)} %bitcast.5, f32[1,256]{1,0:T(1,128)} %dec_hbm.1), custom_call_target="tpu_custom_call" | custom-call | tf_op jit(solution)/shard_map/pallas_call | solution.py:417
  39.5 1.3 %copy.7 = bf16[1,256,32,128]{3,2,1,0:T(8,128)(2,1)} copy(bf16[1,256,32,128]{3,2,1,0:T(8,128)(2,1)S(1)} %bitcast.3) | data formatting | bytes 4194304

commit v6 on v5

--- a/solution.py
+++ b/solution.py
@@ -14,11 +14,13 @@
 WIDTH = 128
 CHIPS = 16
 BAND = CH // CHIPS
-CHUNKS = 4
+CHUNKS = 8
 GROUP = 8
 EARLY = 0
 VMEM_BYTES = 48 << 20
 STEP = HALF // CHUNKS
+RETURNS = 8
+BACK = HALF // RETURNS
 F32 = jnp.float32
 BF16 = jnp.bfloat16
 
@@ -32,7 +34,7 @@
     xp, wc, wo, drive, coef, decs, achip, pair_out, pair_in, merged, up_in, down_out, entry,
     last_out, last_in, y_rows, raw, stage, lines,
     load_sem, halo_s, halo_r, dec_s, dec_r, a_s, a_r, pair_s, pair_r, up_s, up_r,
-    down_s, down_r, last_s, last_r, near_a, near_up, near_down,
+    down_s, down_r, last_s, last_r,
 ):
     tm = lax.axis_index("tm")
     sp = lax.axis_index("space")
@@ -121,6 +123,9 @@
     def first_row(s, q):
         return (1 - s) * (HALF - STEP * (q + 1)) + s * (STEP * q)
 
+    def back_row(s, q):
+        return (1 - s) * (HALF - BACK * (q + 1)) + s * (BACK * q)
+
     lane = lax.broadcasted_iota(jnp.int32, (CH, WIDTH), 1)
 
     def convolved(h):
@@ -140,7 +145,7 @@
         r = first_row(1 - core, q)
         return pltpu.make_async_remote_copy(
             src_ref=pair_out.at[pl.ds(r, STEP)], dst_ref=pair_in.at[pl.ds(r, STEP)],
-            send_sem=pair_s.at[q], recv_sem=pair_r.at[q],
+            send_sem=pair_s, recv_sem=pair_r.at[q],
             device_id={"tm": partner}, device_id_type=MESH,
         )
 
@@ -148,7 +153,7 @@
         r = first_row(core, q)
         return pltpu.make_async_remote_copy(
             src_ref=pair_out.at[pl.ds(r, STEP)], dst_ref=pair_in.at[pl.ds(r, STEP)],
-            send_sem=pair_s.at[q], recv_sem=pair_r.at[q],
+            send_sem=pair_s, recv_sem=pair_r.at[q],
             device_id={"tm": partner}, device_id_type=MESH,
         )
 
@@ -167,7 +172,7 @@
         return pltpu.make_async_remote_copy(
             src_ref=merged.at[pl.ds(r, STEP), pl.ds(pl.multiple_of(to * BAND, BAND), BAND)],
             dst_ref=up_in.at[chip, pl.ds(r, STEP)],
-            send_sem=up_s.at[q], recv_sem=up_r.at[q],
+            send_sem=up_s, recv_sem=up_r.at[q],
             device_id={"tm": to * 2 + core}, device_id_type=MESH,
         )
 
@@ -176,63 +181,48 @@
         return pltpu.make_async_copy(
             merged.at[pl.ds(r, STEP), pl.ds(pl.multiple_of(chip * BAND, BAND), BAND)],
             up_in.at[chip, pl.ds(r, STEP)],
-            near_up.at[q],
+            up_r.at[q],
         )
 
     def down_copy(q, d):
         to = peer(d)
-        r = first_row(core, q)
-        return pltpu.make_async_remote_copy(
-            src_ref=down_out.at[to, pl.ds(r, STEP)],
-            dst_ref=entry.at[pl.ds(r, STEP), pl.ds(pl.multiple_of(chip * BAND, BAND), BAND)],
-            send_sem=down_s.at[q], recv_sem=down_r.at[q],
+        r = back_row(core, q)
+        return pltpu.make_async_remote_copy(
+            src_ref=down_out.at[to, pl.ds(r, BACK)],
+            dst_ref=entry.at[pl.ds(r, BACK), pl.ds(pl.multiple_of(chip * BAND, BAND), BAND)],
+            send_sem=down_s, recv_sem=down_r.at[q],
             device_id={"tm": to * 2 + core}, device_id_type=MESH,
         )
 
     def down_local(q):
-        r = first_row(core, q)
+        r = back_row(core, q)
         return pltpu.make_async_copy(
-            down_out.at[chip, pl.ds(r, STEP)],
-            entry.at[pl.ds(r, STEP), pl.ds(pl.multiple_of(chip * BAND, BAND), BAND)],
-            near_down.at[q],
+            down_out.at[chip, pl.ds(r, BACK)],
+            entry.at[pl.ds(r, BACK), pl.ds(pl.multiple_of(chip * BAND, BAND), BAND)],
+            down_r.at[q],
         )
 
     def last_copy(q):
-        r = first_row(core, q)
-        return pltpu.make_async_remote_copy(
-            src_ref=last_out.at[pl.ds(r, STEP)], dst_ref=last_in.at[pl.ds(r, STEP)],
-            send_sem=last_s.at[q], recv_sem=last_r.at[q],
+        r = back_row(core, q)
+        return pltpu.make_async_remote_copy(
+            src_ref=last_out.at[pl.ds(r, BACK)], dst_ref=last_in.at[pl.ds(r, BACK)],
+            send_sem=last_s, recv_sem=last_r.at[q],
             device_id={"tm": partner}, device_id_type=MESH,
         )
 
     def last_arrival(q):
-        r = first_row(1 - core, q)
-        return pltpu.make_async_remote_copy(
-            src_ref=last_out.at[pl.ds(r, STEP)], dst_ref=last_in.at[pl.ds(r, STEP)],
-            send_sem=last_s.at[q], recv_sem=last_r.at[q],
+        r = back_row(1 - core, q)
+        return pltpu.make_async_remote_copy(
+            src_ref=last_out.at[pl.ds(r, BACK)], dst_ref=last_in.at[pl.ds(r, BACK)],
+            send_sem=last_s, recv_sem=last_r.at[q],
             device_id={"tm": partner}, device_id_type=MESH,
         )
 
-    def a_all():
-        part = achip.at[pl.ds(0, CHIPS - 1)]
-        return pltpu.make_async_remote_copy(
-            src_ref=part, dst_ref=part, send_sem=a_s, recv_sem=a_r,
-            device_id={"tm": partner}, device_id_type=MESH,
-        )
-
-    def up_all(q):
-        part = up_in.at[pl.ds(0, CHIPS - 1), pl.ds(first_row(core, q), STEP)]
-        return pltpu.make_async_remote_copy(
-            src_ref=part, dst_ref=part, send_sem=up_s.at[q], recv_sem=up_r.at[q],
-            device_id={"tm": partner}, device_id_type=MESH,
-        )
-
-    def down_all(q):
-        part = down_out.at[pl.ds(0, CHIPS - 1), pl.ds(first_row(core, q), STEP)]
-        return pltpu.make_async_remote_copy(
-            src_ref=part, dst_ref=part, send_sem=down_s.at[q], recv_sem=down_r.at[q],
-            device_id={"tm": partner}, device_id_type=MESH,
-        )
+    def arrived(part, sem):
+        pltpu.make_async_copy(part, part, sem).wait()
+
+    def sent(part, sem):
+        pltpu.make_async_copy(part, part, sem).wait()
 
     def each(n0, n1, body):
         def run(i, carry):
@@ -257,7 +247,7 @@
             drive[h + e] = driven(ours, e)
 
     a_local = pltpu.make_async_copy(
-        coef.at[5, pl.ds(pl.multiple_of(chip * BAND, BAND), BAND)], achip.at[chip], near_a
+        coef.at[5, pl.ds(pl.multiple_of(chip * BAND, BAND), BAND)], achip.at[chip], a_r
     )
 
     def coefficients():
@@ -285,16 +275,19 @@
         up_local(q).start()
 
     def scan(q):
-        up_all(q).wait_recv()
-        up_local(q).wait()
+        arrived(up_in.at[:, pl.ds(first_row(core, q), STEP)], up_r.at[q])
         rows = pl.ds(first_row(core, q), STEP)
         state = jnp.zeros((STEP, BAND, WIDTH), F32)
         for i in range(CHIPS):
             down_out[i, rows] = state.astype(BF16)
             if i < CHIPS - 1:
                 state = achip[i][None] * state + up_in[i, rows].astype(F32)
-        each(1, CHIPS, lambda d: down_copy(q, d).start())
-        down_local(q).start()
+
+        def give(p):
+            each(1, CHIPS, lambda d: down_copy(p, d).start())
+            down_local(p).start()
+
+        each(STEP // BACK * q, STEP // BACK * (q + 1), give)
 
     reorder(1)
     reorder(2)
@@ -341,8 +334,7 @@
             merge_half(q - 1)
 
     each(1, CHUNKS, front)
-    a_all().wait()
-    a_local.wait()
+    arrived(achip, a_r)
     each(0, EARLY, scan)
     merge_half(CHUNKS - 1)
     each(EARLY, CHUNKS, scan)
@@ -358,19 +350,16 @@
             )
 
     def put(s, q):
-        @pl.when(lax.rem(q, GROUP // STEP) == GROUP // STEP - 1)
+        @pl.when(lax.rem(q, GROUP // BACK) == GROUP // BACK - 1)
         def _():
-            b = (first_row(s, q) + HALF * s) // GROUP
+            b = (back_row(s, q) + HALF * s) // GROUP
             y_out[:, pl.ds(pl.multiple_of(b * GROUP, GROUP), GROUP)] = (
                 y_rows[b].reshape(CH, GROUP, WIDTH).astype(BF16)
             )
 
-    def finish(q):
-        pair_copy(q).wait_send()
-        up_all(q).wait_send()
-        down_all(q).wait_recv()
-        down_local(q).wait()
-        r0 = first_row(core, q)
+    def finish_own(q):
+        arrived(entry.at[pl.ds(back_row(core, q), BACK)], down_r.at[q])
+        r0 = back_row(core, q)
 
         def answer(e):
             r = r0 + e
@@ -379,20 +368,22 @@
             drive[r + HALF * core] = memory
             last_out[r] = ((1.0 - second) * memory + second * enter).astype(BF16)
 
-        each(0, STEP, answer)
+        each(0, BACK, answer)
         last_copy(q).start()
 
-        def own_tile(t):
+        def tile(t):
             h = r0 + 2 * t + HALF * core
             project(h, [drive[h + e].astype(BF16) for e in range(2)])
 
-        each(0, STEP // 2, own_tile)
+        each(0, BACK // 2, tile)
         put(core, q)
+
+    def finish_other(q):
         last_arrival(q).wait_recv()
-        r1 = first_row(other, q)
-
-        def other_tile(t):
-            r = r1 + 2 * t
+        r0 = back_row(other, q)
+
+        def tile(t):
+            r = r0 + 2 * t
             h = r + HALF * other
             project(
                 h,
@@ -402,12 +393,24 @@
                 ],
             )
 
-        each(0, STEP // 2, other_tile)
+        each(0, BACK // 2, tile)
         put(other, q)
-        last_copy(q).wait_send()
-        down_all(q).wait_send()
-
-    each(0, CHUNKS, finish)
+
+    def finish(q):
+        @pl.when(q < RETURNS)
+        def _():
+            finish_own(q)
+
+        @pl.when(q > 0)
+        def _():
+            finish_other(q - 1)
+
+    each(0, RETURNS + 1, finish)
+    sent(pair_out, pair_s)
+    sent(last_out, last_s)
+    sent(achip.at[pl.ds(0, CHIPS - 1)], a_s)
+    sent(up_in.at[pl.ds(0, CHIPS - 1)], up_s)
+    sent(down_out.at[pl.ds(0, CHIPS - 1)], down_s)
 
 
 def on_device(frames_in, conv_weight, out_weight, skip_gain, decays):
@@ -446,17 +449,14 @@
             dma,
             dma,
             dma,
+            dma,
             dma((CHUNKS,)),
+            dma,
             dma((CHUNKS,)),
-            dma((CHUNKS,)),
-            dma((CHUNKS,)),
-            dma((CHUNKS,)),
-            dma((CHUNKS,)),
-            dma((CHUNKS,)),
-            dma((CHUNKS,)),
-            dma,
-            dma((CHUNKS,)),
-            dma((CHUNKS,)),
+            dma,
+            dma((RETURNS,)),
+            dma,
+            dma((RETURNS,)),
         ],
         compiler_params=pltpu.CompilerParams(
             collective_id=0, has_side_effects=True, vmem_limit_bytes=VMEM_BYTES

time: 41 us -> 40.1 us (0.978)
  Pallas kernels: 39.5 us -> 38.6 us
    pallas_call x1, Pallas kernels: 39.5 us -> 38.6 us  [on_device(): pl.pallas_call(kernel, out_shape=jax.ShapeDtypeStruct((CH, ROWS, WIDTH),...]
where the time goes in v6:
time: 40.1 us; the launch traced here: 40 us
  Pallas kernels  38.6 us (96%)
  local copies, waits for them, and re-layouts  1.32 us (3%)
    pallas_call x1, Pallas kernels, on_device(): pl.pallas_call(kernel, out_shape=jax.ShapeDtypeStruct((CH, ROWS, WIDTH),...  38.6 us
    unnamed x1, local copies, waits for them, and re-layouts  1.32 us

profile of v6, /device:TPU:1, one launch (start us, length us, event | category | flops | bytes accessed | tf_op | source)
XLA Modules:
  0.0 40.0 jit_solution(7410544324826830256)
XLA Ops:
  0.0 38.6 %shard_map.55 = bf16[256,32,128]{2,1,0:T(8,128)(2,1)S(1)} custom-call(bf16[256,32,128]{2,1,0:T(8,128)(2,1)} %bitcast.4, bf16[3,3,256,256]{3,2,1,0:T(8,128)(2,1)} %w_hbm.1, bf16[256,256]{1,0:T(8,128)(2,1)} %wo_hbm.1, f32[1,256]{1,0:T(1,128)} %bitcast.5, f32[1,256]{1,0:T(1,128)} %dec_hbm.1), custom_call_target="tpu_custom_call" | custom-call | tf_op jit(solution)/shard_map/pallas_call | solution.py:420
  38.7 1.3 %copy.7 = bf16[1,256,32,128]{3,2,1,0:T(8,128)(2,1)} copy(bf16[1,256,32,128]{3,2,1,0:T(8,128)(2,1)S(1)} %bitcast.3) | data formatting | bytes 4194304

commit v7 on v6

--- a/solution.py
+++ b/solution.py
@@ -293,14 +293,9 @@
     reorder(2)
     pltpu.make_async_copy(wc, wc, load_sem.at[5]).wait()
     each(0, STEP // 2, lambda t: conv_tile(0, t))
-    reorder(0)
-    reorder(3)
-    wo_load.wait()
     pl.semaphore_wait(barrier, CHIPS + 2)
     dec_copy.start()
     pair_copy(0).start()
-    halo(0).start()
-    halo(1).start()
 
     def front(q):
         @pl.when(q == CHUNKS - 1)
@@ -328,6 +323,14 @@
 
         each(0, STEP // 2, step)
         pair_copy(q).start()
+
+        @pl.when(q == 1)
+        def _():
+            reorder(0)
+            reorder(3)
+            halo(0).start()
+            halo(1).start()
+            wo_load.wait()
 
         @pl.when(q > 1)
         def _():

time: 40.1 us -> 39.7 us (0.990)
  no operation moved by 1% of the time
where the time goes in v7:
time: 39.7 us; the launch traced here: 39.6 us
  Pallas kernels  38.3 us (96%)
  local copies, waits for them, and re-layouts  1.32 us (3%)
    pallas_call x1, Pallas kernels, on_device(): pl.pallas_call(kernel, out_shape=jax.ShapeDtypeStruct((CH, ROWS, WIDTH),...  38.3 us
    unnamed x1, local copies, waits for them, and re-layouts  1.32 us

profile of v7, /device:TPU:1, one launch (start us, length us, event | category | flops | bytes accessed | tf_op | source)
XLA Modules:
  0.0 39.6 jit_solution(5320433296585006018)
XLA Ops:
  0.0 38.3 %shard_map.55 = bf16[256,32,128]{2,1,0:T(8,128)(2,1)S(1)} custom-call(bf16[256,32,128]{2,1,0:T(8,128)(2,1)} %bitcast.4, bf16[3,3,256,256]{3,2,1,0:T(8,128)(2,1)} %w_hbm.1, bf16[256,256]{1,0:T(8,128)(2,1)} %wo_hbm.1, f32[1,256]{1,0:T(1,128)} %bitcast.5, f32[1,256]{1,0:T(1,128)} %dec_hbm.1), custom_call_target="tpu_custom_call" | custom-call | tf_op jit(solution)/shard_map/pallas_call | solution.py:423
  38.3 1.3 %copy.7 = bf16[1,256,32,128]{3,2,1,0:T(8,128)(2,1)} copy(bf16[1,256,32,128]{3,2,1,0:T(8,128)(2,1)S(1)} %bitcast.3) | data formatting | bytes 4194304

commit v8 on v7

--- a/solution.py
+++ b/solution.py
@@ -46,19 +46,6 @@
 
     def peer(d):
         return lax.rem(chip + d, CHIPS)
-
-    barrier = pltpu.get_barrier_semaphore()
-
-    def greet(d, carry):
-        pl.semaphore_signal(
-            barrier, inc=1, device_id={"tm": peer(d) * 2 + core}, device_id_type=MESH
-        )
-        return carry
-
-    pl.semaphore_signal(barrier, inc=1, device_id={"tm": partner}, device_id_type=MESH)
-    pl.semaphore_signal(barrier, inc=1, device_id={"space": above}, device_id_type=MESH)
-    pl.semaphore_signal(barrier, inc=1, device_id={"space": below}, device_id_type=MESH)
-    lax.fori_loop(1, CHIPS, greet, 0)
 
     x_loads = [
         pltpu.make_async_copy(
@@ -91,6 +78,19 @@
     x_loads[3].start()
     wo_load.start()
 
+    barrier = pltpu.get_barrier_semaphore()
+
+    def greet(d, carry):
+        pl.semaphore_signal(
+            barrier, inc=1, device_id={"tm": peer(d) * 2 + core}, device_id_type=MESH
+        )
+        return carry
+
+    pl.semaphore_signal(barrier, inc=1, device_id={"tm": partner}, device_id_type=MESH)
+    pl.semaphore_signal(barrier, inc=1, device_id={"space": above}, device_id_type=MESH)
+    pl.semaphore_signal(barrier, inc=1, device_id={"space": below}, device_id_type=MESH)
+    lax.fori_loop(1, CHIPS, greet, 0, unroll=True)
+
     for load in small_loads:
         load.wait()
     own_decay = column(lines[0])
@@ -271,7 +271,8 @@
             drive[r + HALF * core] = (1.0 - second) * own + second * total
 
         each(0, STEP, merge)
-        each(1, CHIPS, lambda d: up_copy(q, d).start())
+        for d in range(1, CHIPS):
+            up_copy(q, d).start()
         up_local(q).start()
 
     def scan(q):
@@ -284,7 +285,8 @@
                 state = achip[i][None] * state + up_in[i, rows].astype(F32)
 
         def give(p):
-            each(1, CHIPS, lambda d: down_copy(p, d).start())
+            for d in range(1, CHIPS):
+                down_copy(p, d).start()
             down_local(p).start()
 
         each(STEP // BACK * q, STEP // BACK * (q + 1), give)

time: 39.7 us -> 39.7 us (level)
  no operation moved by 1% of the time
where the time goes in v8:
time: 39.7 us; the launch traced here: 39.6 us
  Pallas kernels  38.3 us (96%)
  local copies, waits for them, and re-layouts  1.32 us (3%)
    pallas_call x1, Pallas kernels, on_device(): pl.pallas_call(kernel, out_shape=jax.ShapeDtypeStruct((CH, ROWS, WIDTH),...  38.3 us
    unnamed x1, local copies, waits for them, and re-layouts  1.32 us

profile of v8, /device:TPU:1, one launch (start us, length us, event | category | flops | bytes accessed | tf_op | source)
XLA Modules:
  0.0 39.6 jit_solution(14959273662792329944)
XLA Ops:
  0.0 38.3 %shard_map.55 = bf16[256,32,128]{2,1,0:T(8,128)(2,1)S(1)} custom-call(bf16[256,32,128]{2,1,0:T(8,128)(2,1)} %bitcast.4, bf16[3,3,256,256]{3,2,1,0:T(8,128)(2,1)} %w_hbm.1, bf16[256,256]{1,0:T(8,128)(2,1)} %wo_hbm.1, f32[1,256]{1,0:T(1,128)} %bitcast.5, f32[1,256]{1,0:T(1,128)} %dec_hbm.1), custom_call_target="tpu_custom_call" | custom-call | tf_op jit(solution)/shard_map/pallas_call | solution.py:425
  38.3 1.3 %copy.7 = bf16[1,256,32,128]{3,2,1,0:T(8,128)(2,1)} copy(bf16[1,256,32,128]{3,2,1,0:T(8,128)(2,1)S(1)} %bitcast.3) | data formatting | bytes 4194304

commit v9 on v8

--- a/solution.py
+++ b/solution.py
@@ -16,7 +16,7 @@
 BAND = CH // CHIPS
 CHUNKS = 8
 GROUP = 8
-EARLY = 0
+EARLY = 1
 VMEM_BYTES = 48 << 20
 STEP = HALF // CHUNKS
 RETURNS = 8

time: 39.7 us -> 39.7 us (level)
  no operation moved by 1% of the time
where the time goes in v9:
time: 39.7 us; the launch traced here: 39.6 us
  Pallas kernels  38.3 us (96%)
  local copies, waits for them, and re-layouts  1.32 us (3%)
    pallas_call x1, Pallas kernels, on_device(): pl.pallas_call(kernel, out_shape=jax.ShapeDtypeStruct((CH, ROWS, WIDTH),...  38.3 us
    unnamed x1, local copies, waits for them, and re-layouts  1.32 us

profile of v9, /device:TPU:1, one launch (start us, length us, event | category | flops | bytes accessed | tf_op | source)
XLA Modules:
  0.0 39.6 jit_solution(7073844778576364128)
XLA Ops:
  0.0 38.3 %shard_map.55 = bf16[256,32,128]{2,1,0:T(8,128)(2,1)S(1)} custom-call(bf16[256,32,128]{2,1,0:T(8,128)(2,1)} %bitcast.4, bf16[3,3,256,256]{3,2,1,0:T(8,128)(2,1)} %w_hbm.1, bf16[256,256]{1,0:T(8,128)(2,1)} %wo_hbm.1, f32[1,256]{1,0:T(1,128)} %bitcast.5, f32[1,256]{1,0:T(1,128)} %dec_hbm.1), custom_call_target="tpu_custom_call" | custom-call | tf_op jit(solution)/shard_map/pallas_call | solution.py:425
  38.3 1.3 %copy.7 = bf16[1,256,32,128]{3,2,1,0:T(8,128)(2,1)} copy(bf16[1,256,32,128]{3,2,1,0:T(8,128)(2,1)S(1)} %bitcast.3) | data formatting | bytes 4194304
